TPU v7x, 128 devices: a whole 4x4x4 slice. The times are simulated.
128 devices in a mesh: seg: 16 (over x, y), head: 8 (over z, core).
Axes of the slice: x: 4, y: 4, z: 4, core: 2. Of those that a mesh axis runs over, the one named last changes fastest.
Arguments:
- query_feat: float32 [1792, 51200], P('head', 'seg'), may hold values from -6 to 6
- key_feat: float32 [1792, 51200], P('head', 'seg'), may hold values from -6 to 6
- value_feat: float32 [1792, 51200], P('head', 'seg'), may hold values from -5.5 to 5.5
- grad_out: float32 [1792, 51200], P('head', 'seg'), may hold values from -6 to 6
- spatial_weight: float32 [3, 3, 1792], replicated, may hold values from -2 to 2
- temporal_weight: float32 [3, 1792], replicated, may hold values from -3.5 to 3.5
Outputs:
- grad_query: float32 [1792, 51200], P('head', 'seg')
- grad_key: float32 [1792, 51200], P('head', 'seg')
- grad_value: float32 [1792, 51200], P('head', 'seg')
- mixed: float32 [64, 20, 40, 1792], P('seg', None, 'head')
All inputs are finite; a program needn't handle non-finite values.
Results may differ from a plain program's by a relative error of at most 0.00008.
Values sent between devices are 32-bit elements; how exact they have to be, the bound alone decides.
A program may use at most 128 MiB of HBM per device.

v0:
```python
import functools

import jax
import jax.numpy as jnp
from jax import lax
from jax.experimental import pallas as pl
from jax.experimental.pallas import tpu as pltpu
from jax.sharding import PartitionSpec as P

D = 112
ROWS = 20
COLS = 40
FRAMES = 4
STRIDE = 768
WIN = 896
HEADS = 2
STRIPS = 8
CELLS = 100
CHUNKS = ((0, 256), (256, 256), (512, 256), (768, 128))
BASE = 136
MESH = pl.DeviceIdType.MESH
F32 = jnp.float32
BF16 = jnp.bfloat16
VMEM_LIMIT = 60 * 1024 * 1024


def split(x):
    hi = x.astype(BF16)
    lo = (x - hi.astype(F32)).astype(BF16)
    return hi, lo


def nn(a, b):
    return lax.dot_general(a, b, (((1,), (0,)), ((), ())), preferred_element_type=F32)


def nt(a, b):
    return lax.dot_general(a, b, (((1,), (1,)), ((), ())), preferred_element_type=F32)


def pad_rows(x):
    return jnp.concatenate([x, jnp.zeros((16, x.shape[1]), x.dtype)], axis=0)


def left_mul(pair, b_hi, b_lo):
    return nn(pair, jnp.concatenate([b_hi, b_hi], axis=0)) + nn(pair[:, :128], b_lo)


def outer(a_hi, a_lo, b_hi, b_lo):
    both = nt(jnp.concatenate([a_hi, a_lo], axis=0), b_hi)
    rows = a_hi.shape[0]
    return both[:rows] + both[rows:] + nt(a_hi, b_lo)


def in_frame(frame, start, width):
    lane = lax.broadcasted_iota(jnp.int32, (1, width), 1) + start
    return (lane >= 32 * frame) & (lane < 32 * frame + ROWS * COLS)


def extra_row(row):
    place = lax.broadcasted_iota(jnp.int32, (16, row.shape[1]), 0)
    return jnp.where(place == 0, jnp.broadcast_to(row, (16, row.shape[1])), 0.0)


def side_by_side(x):
    hi, lo = split(x)
    return jnp.concatenate([hi, lo], axis=1)


def sums_kernel(k_ref, v_ref, out_ref, k_win, v_win, sem):
    def copies(h, f):
        rows = pl.ds(D * h, D)
        lanes = pl.ds(STRIDE * f, WIN)
        return (
            pltpu.make_async_copy(k_ref.at[rows, lanes], k_win.at[h, f], sem.at[0, h, f]),
            pltpu.make_async_copy(v_ref.at[rows, lanes], v_win.at[h, f], sem.at[1, h, f]),
        )

    for h in range(HEADS):
        for f in range(FRAMES):
            for c in copies(h, f):
                c.start()
    for h in range(HEADS):
        def one(f, total, h=h):
            for c in copies(h, f):
                c.wait()
            for start, width in CHUNKS:
                lanes = slice(start, start + width)
                ok = in_frame(f, start, width)
                k_hi, k_lo = split(jnp.where(ok, jnp.exp(k_win[h, f, :, lanes]), 0.0))
                v_hi, v_lo = split(v_win[h, f, :, lanes])
                ones = extra_row(jnp.ones((1, width), F32)).astype(BF16)
                v_hi = jnp.concatenate([v_hi, ones], axis=0)
                total = total + outer(k_hi, k_lo, v_hi, pad_rows(v_lo))
            out_ref[h, f] = total
            return total

        lax.fori_loop(0, FRAMES, one, jnp.zeros((D, 128), F32))


def key_value_sums(key_feat, value_feat):
    return pl.pallas_call(
        sums_kernel,
        out_shape=jax.ShapeDtypeStruct((HEADS, FRAMES, D, 128), F32),
        in_specs=[pl.BlockSpec(memory_space=pl.ANY)] * 2,
        out_specs=pl.BlockSpec(memory_space=pltpu.VMEM),
        scratch_shapes=[
            pltpu.VMEM((HEADS, FRAMES, D, WIN), F32),
            pltpu.VMEM((HEADS, FRAMES, D, WIN), F32),
            pltpu.SemaphoreType.DMA((2, HEADS, FRAMES)),
        ],
        compiler_params=pltpu.CompilerParams(vmem_limit_bytes=VMEM_LIMIT),
        name="key_value_sums",
    )(key_feat, value_feat)


def greet(devices):
    barrier = pltpu.get_barrier_semaphore()
    for dev in devices:
        pl.semaphore_signal(barrier, inc=1, device_id=dev, device_id_type=MESH)
    pl.semaphore_wait(barrier, len(devices))


def scan_peers():
    seg, head = lax.axis_index("seg"), lax.axis_index("head")
    x, y = seg // 4, seg % 4
    along_y = [(x * 4 + (y + k) % 4, head) for k in range(1, 4)]
    along_x = [(((x + k) % 4) * 4 + y, head) for k in range(1, 4)]
    return along_y, along_x


SCAN_SCRATCH = [
    pltpu.VMEM((4, 56, 128), F32),
    pltpu.VMEM((56, 128), F32),
    pltpu.VMEM((4, 56, 128), F32),
    pltpu.VMEM((4, 56, 128), F32),
    pltpu.SemaphoreType.DMA((3, 4)),
    pltpu.SemaphoreType.DMA((3, 4)),
]


class Scan:
    def __init__(self, own, result, scratch, reverse):
        self.own, self.result, self.reverse = own, result, reverse
        self.got, self.line, self.lines, self.back, self.send, self.recv = scratch
        seg = lax.axis_index("seg")
        self.x, self.y = seg // 4, seg % 4
        self.along_y, self.along_x = scan_peers()

    def copy(self, phase, k, src, dst, dev):
        return pltpu.make_async_remote_copy(
            src_ref=src, dst_ref=dst, send_sem=self.send.at[phase, k], recv_sem=self.recv.at[phase, k],
            device_id=dev, device_id_type=MESH,
        )

    def first(self):
        self.c1 = [
            self.copy(0, k, self.own.at[(self.y + k) % 4], self.got.at[k], self.along_y[k - 1])
            for k in range(1, 4)
        ]
        for c in self.c1:
            c.start()

    def second(self):
        for c in self.c1:
            c.wait()
        mine = self.own[self.y]
        self.line[...] = mine + self.got[1] + self.got[2] + self.got[3]
        self.c2 = [
            self.copy(1, k, self.line, self.lines.at[k], self.along_x[k - 1]) for k in range(1, 4)
        ]
        for c in self.c2:
            c.start()

    def counts(self, place, source):
        return source > place if self.reverse else source < place

    def third(self):
        for c in self.c2:
            c.wait()
        zero = jnp.zeros((56, 128), F32)
        before = zero
        for k in range(1, 4):
            source = (self.x + 4 - k) % 4
            before = before + jnp.where(self.counts(self.x, source), self.lines[k], zero)
        terms = [(self.y, self.own[self.y])] + [((self.y + 4 - k) % 4, self.got[k]) for k in range(1, 4)]
        for k in range(4):
            target = (self.y + k) % 4
            total = before
            for source, value in terms:
                total = total + jnp.where(self.counts(target, source), value, zero)
            self.back[k] = total
        self.c3 = [
            self.copy(2, k, self.back.at[k], self.result.at[self.y], self.along_y[k - 1]) for k in range(1, 4)
        ]
        for c in self.c3:
            c.start()
        self.result[self.y] = self.back[0]

    def last(self):
        for c in self.c3:
            c.wait()


def scan_kernel(own_ref, out_ref, result, *scratch):
    along_y, along_x = scan_peers()
    greet(along_y + along_x)
    scan = Scan(own_ref, result, scratch, False)
    scan.first()
    scan.second()
    scan.third()
    scan.last()
    out_ref[...] = result[...]


def prefix(own):
    return pl.pallas_call(
        scan_kernel,
        out_shape=jax.ShapeDtypeStruct((4, 56, 128), F32),
        in_specs=[pl.BlockSpec(memory_space=pltpu.VMEM)],
        out_specs=pl.BlockSpec(memory_space=pltpu.VMEM),
        scratch_shapes=[pltpu.VMEM((4, 56, 128), F32)] + SCAN_SCRATCH,
        compiler_params=pltpu.CompilerParams(collective_id=0, has_side_effects=True),
        name="prefix",
    )(own)


def state_of(before_ref, local_ref, h, f):
    return before_ref[h] + local_ref[h, f]


def query_frame(f, q_win, g_win, before_ref, local_ref, gq_ref, ds_ref, att, conv_in, w_ref, send_ref):
    for h in range(HEADS):
        state = state_of(before_ref, local_ref, h, f)
        plain = side_by_side(state)
        turned = side_by_side(pad_rows(state).T)
        rows = slice(D * h, D * h + D)
        grad_state = jnp.zeros((D, 128), F32)
        for start, width in CHUNKS:
            lanes = slice(start, start + width)
            ok = in_frame(f, start, width)
            feat = jnp.exp(q_win[f, rows, lanes])
            q_hi, q_lo = split(feat)
            numer = left_mul(turned, pad_rows(q_hi), pad_rows(q_lo))
            inverse = 1.0 / numer[D:D + 1]
            attended = numer[:D] * inverse
            att[rows, lanes] = jnp.where(ok, attended, 0.0)
            grad = g_win[f, rows, lanes]
            slope = -jnp.sum(grad * attended, axis=0, keepdims=True) * inverse
            ext = jnp.where(ok, jnp.concatenate([grad * inverse, extra_row(slope)], axis=0), 0.0)
            n_hi, n_lo = split(ext)
            gq = left_mul(plain, n_hi, n_lo) * feat
            place = pl.ds(pl.multiple_of(STRIDE * f + start, 128), width)
            gq_ref[rows, place] = jnp.where(ok, gq, gq_ref[rows, place])
            grad_state = grad_state + outer(q_hi, q_lo, n_hi, n_lo)
        ds_ref[h, f] = grad_state
    for m in range(WIN // 128):
        place = pl.ds(pl.multiple_of(BASE - 32 * f + 128 * m, 8), 128)
        conv_in[place, :] = att[:, 128 * m:128 * m + 128].T
    edge = lax.broadcasted_iota(jnp.int32, (COLS, 128), 0)
    for lane in range(2):
        lanes = slice(128 * lane, 128 * lane + 128)
        taps = [[w_ref[3 * i + j:3 * i + j + 1, lanes] for j in range(3)] for i in range(3)]
        for r in range(ROWS):
            lines = [conv_in[BASE + COLS * (r + i - 1):BASE + COLS * (r + i), lanes] for i in range(3)]
            cols = [taps[0][j] * lines[0] + taps[1][j] * lines[1] + taps[2][j] * lines[2] for j in range(3)]
            total = (
                cols[1]
                + jnp.where(edge == 0, 0.0, pltpu.roll(cols[0], 1, 0))
                + jnp.where(edge == COLS - 1, 0.0, pltpu.roll(cols[2], COLS - 1, 0))
            )
            half = 0.5 * total
            act = half + half * jnp.tanh(half)
            for j in range(STRIPS):
                send_ref[f, j, 5 * r:5 * r + 5, lanes] = act[5 * j:5 * j + 5]


def query_kernel(q_ref, g_ref, before_ref, local_ref, w_ref, gq_ref, ds_ref, send_ref, q_win, g_win, att, conv_in, sem):
    def copies(f):
        lanes = pl.ds(STRIDE * f, WIN)
        return (
            pltpu.make_async_copy(q_ref.at[:, lanes], q_win.at[f], sem.at[0, f]),
            pltpu.make_async_copy(g_ref.at[:, lanes], g_win.at[f], sem.at[1, f]),
        )

    for f in range(FRAMES):
        for c in copies(f):
            c.start()
    att[...] = jnp.zeros_like(att)
    conv_in[...] = jnp.zeros_like(conv_in)

    def one(f, carry):
        for c in copies(f):
            c.wait()
        query_frame(f, q_win, g_win, before_ref, local_ref, gq_ref, ds_ref, att, conv_in, w_ref, send_ref)
        return carry

    lax.fori_loop(0, FRAMES, one, 0)
    for h in range(HEADS):
        for f in range(FRAMES - 2, -1, -1):
            ds_ref[h, f] = ds_ref[h, f] + ds_ref[h, f + 1]


def query_side(q, g, before, local, weights):
    vmem = pl.BlockSpec(memory_space=pltpu.VMEM)
    return pl.pallas_call(
        query_kernel,
        out_shape=(
            jax.ShapeDtypeStruct((HEADS * D, STRIDE * 3 + WIN), F32),
            jax.ShapeDtypeStruct((HEADS, FRAMES, D, 128), F32),
            jax.ShapeDtypeStruct((FRAMES, STRIPS, CELLS, 256), F32),
        ),
        in_specs=[pl.BlockSpec(memory_space=pl.ANY)] * 2 + [vmem] * 3,
        out_specs=(vmem, vmem, vmem),
        scratch_shapes=[
            pltpu.VMEM((FRAMES, HEADS * D, WIN), F32),
            pltpu.VMEM((FRAMES, HEADS * D, WIN), F32),
            pltpu.VMEM((256, WIN), F32),
            pltpu.VMEM((BASE + WIN, 256), F32),
            pltpu.SemaphoreType.DMA((2, FRAMES)),
        ],
        compiler_params=pltpu.CompilerParams(vmem_limit_bytes=VMEM_LIMIT),
        name="query_side",
    )(q, g, before, local, weights)


ORDER = (2, 3, 0, 1)
HOPS = (1, 2, 6, 3, 5, 7, 4)


def exchange_kernel(act_ref, own_ref, got_ref, halo_ref, after_ref, result, send, recv, fsend, frecv, lsem, *scratch):
    seg, head = lax.axis_index("seg"), lax.axis_index("head")
    along_y, along_x = scan_peers()
    peers = [(seg, head ^ k) for k in range(1, 8)]
    up, down = ((seg + 1) % 16, head), ((seg + 15) % 16, head)
    barrier = pltpu.get_barrier_semaphore()
    for dev in along_y + along_x + peers + [up, down]:
        pl.semaphore_signal(barrier, inc=1, device_id=dev, device_id_type=MESH)
    pl.semaphore_wait(barrier, 15)

    def strip(f, k):
        return pltpu.make_async_remote_copy(
            src_ref=act_ref.at[f, head ^ k], dst_ref=got_ref.at[k, f], send_sem=send.at[f, k], recv_sem=recv.at[f, k],
            device_id=(seg, head ^ k), device_id_type=MESH,
        )

    def forward(f, k):
        src = act_ref.at[f, head] if k == 0 else got_ref.at[k, f]
        return pltpu.make_async_remote_copy(
            src_ref=src, dst_ref=halo_ref.at[k, f - 2], send_sem=fsend.at[f - 2, k], recv_sem=frecv.at[f - 2, k],
            device_id=up, device_id_type=MESH,
        )

    scan = Scan(own_ref, result, scratch, True)
    scan.first()
    for f in ORDER:
        for k in HOPS:
            strip(f, k).start()
    for f in (2, 3):
        forward(f, 0).start()
    for f in range(FRAMES):
        pltpu.make_async_copy(act_ref.at[f, head], got_ref.at[0, f], lsem.at[f]).start()
    scan.second()
    scan.third()
    scan.last()
    after_ref[...] = result[...]
    for f in (2, 3):
        for k in HOPS:
            strip(f, k).wait_recv()
            forward(f, k).start()
    for f in range(FRAMES):
        pltpu.make_async_copy(act_ref.at[f, head], got_ref.at[0, f], lsem.at[f]).wait()
    for f in (0, 1):
        for k in HOPS:
            strip(f, k).wait_recv()
    for f in ORDER:
        for k in HOPS:
            strip(f, k).wait_send()
    for f in (2, 3):
        for k in (0,) + HOPS:
            forward(f, k).wait()


def exchange(act, own):
    hbm = pl.BlockSpec(memory_space=pl.ANY)
    vmem = pl.BlockSpec(memory_space=pltpu.VMEM)
    return pl.pallas_call(
        exchange_kernel,
        out_shape=(
            jax.ShapeDtypeStruct((STRIPS, FRAMES, CELLS, 256), F32),
            jax.ShapeDtypeStruct((STRIPS, 2, CELLS, 256), F32),
            jax.ShapeDtypeStruct((4, 56, 128), F32),
        ),
        in_specs=[hbm, vmem],
        out_specs=(hbm, hbm, vmem),
        scratch_shapes=[
            pltpu.VMEM((4, 56, 128), F32),
            pltpu.SemaphoreType.DMA((FRAMES, 8)),
            pltpu.SemaphoreType.DMA((FRAMES, 8)),
            pltpu.SemaphoreType.DMA((2, 8)),
            pltpu.SemaphoreType.DMA((2, 8)),
            pltpu.SemaphoreType.DMA((FRAMES,)),
        ] + SCAN_SCRATCH,
        compiler_params=pltpu.CompilerParams(collective_id=1, has_side_effects=True, vmem_limit_bytes=8 << 20),
        name="exchange",
    )(act, own)


def mix_group(base, count, halo_on, got, halo, tw_ref, tmp, mixed_ref):
    head = lax.axis_index("head")
    place = lax.broadcasted_iota(jnp.int32, (count, 128), 1)
    pending = [None] * FRAMES
    for owner in range(STRIPS):
        slot = head ^ owner
        for lane in range(2):
            lanes = slice(128 * lane, 128 * lane + 128)
            acts = [jnp.where(halo_on, halo[slot, i, pl.ds(base, count), lanes], 0.0) for i in range(2)]
            acts += [got[slot, f, pl.ds(base, count), lanes] for f in range(FRAMES)]
            w = [tw_ref[owner, i:i + 1, lanes] for i in range(3)]
            width = 128 if lane == 0 else 96
            tile, shift = divmod(224 * owner + 128 * lane, 128)
            for f in range(FRAMES):
                val = w[0] * acts[f + 2] + w[1] * acts[f + 1] + w[2] * acts[f]
                full = val
                if shift:
                    val = pltpu.roll(val, shift, 1)
                    full = jnp.where(place < shift, pending[f], val)
                if shift + width >= 128:
                    tmp[tile, pl.ds(f, count, stride=4), :] = full
                    pending[f] = val
                else:
                    pending[f] = full


def key_kernel(k_ref, v_ref, after_ref, local_ref, got_hbm, halo_hbm, tw_ref, gk_ref, gv_ref, mixed_ref,
               k_win, v_win, got, halo, tmp, sem, sem2):
    def copies(f):
        lanes = pl.ds(STRIDE * f, WIN)
        return (
            pltpu.make_async_copy(k_ref.at[:, lanes], k_win.at[f], sem.at[0, f]),
            pltpu.make_async_copy(v_ref.at[:, lanes], v_win.at[f], sem.at[1, f]),
        )

    for f in range(FRAMES):
        for c in copies(f):
            c.start()
    got_copy = pltpu.make_async_copy(got_hbm, got, sem2.at[0])
    halo_copy = pltpu.make_async_copy(halo_hbm, halo, sem2.at[1])
    got_copy.start()
    halo_copy.start()

    def one(f, carry):
        for c in copies(f):
            c.wait()
        for h in range(HEADS):
            state = state_of(after_ref, local_ref, h, f)
            plain = side_by_side(state)
            turned = side_by_side(pad_rows(state).T)
            rows = slice(D * h, D * h + D)
            for start, width in CHUNKS:
                lanes = slice(start, start + width)
                ok = in_frame(f, start, width)
                feat = jnp.exp(k_win[f, rows, lanes])
                k_hi, k_lo = split(feat)
                v_hi, v_lo = split(v_win[f, rows, lanes])
                ones = extra_row(jnp.ones((1, width), F32)).astype(BF16)
                v_hi = jnp.concatenate([v_hi, ones], axis=0)
                gk = left_mul(plain, v_hi, pad_rows(v_lo)) * feat
                gv = left_mul(turned, pad_rows(k_hi), pad_rows(k_lo))[:D]
                place = pl.ds(pl.multiple_of(STRIDE * f + start, 128), width)
                gk_ref[rows, place] = jnp.where(ok, gk, gk_ref[rows, place])
                gv_ref[rows, place] = jnp.where(ok, gv, gv_ref[rows, place])
        return carry

    lax.fori_loop(0, FRAMES, one, 0)
    got_copy.wait()
    halo_copy.wait()
    halo_on = lax.axis_index("seg") > 0

    def group(base, count):
        mix_group(base, count, halo_on, got, halo, tw_ref, tmp, mixed_ref)
        for i in range(count):
            for t in range(14):
                mixed_ref[base + i, :, 128 * t:128 * t + 128] = tmp[t, 4 * i:4 * i + 4, :]

    def step(i, carry):
        group(pl.multiple_of(8 * i, 8), 8)
        return carry

    lax.fori_loop(0, 12, step, 0)
    group(96, 4)


def key_side(k, v, after, local, got, halo, tw):
    vmem = pl.BlockSpec(memory_space=pltpu.VMEM)
    hbm = pl.BlockSpec(memory_space=pl.ANY)
    return pl.pallas_call(
        key_kernel,
        out_shape=(
            jax.ShapeDtypeStruct((HEADS * D, 3200), F32),
            jax.ShapeDtypeStruct((HEADS * D, 3200), F32),
            jax.ShapeDtypeStruct((CELLS, FRAMES, 1792), F32),
        ),
        in_specs=[hbm, hbm, vmem, vmem, hbm, hbm, vmem],
        out_specs=(vmem, vmem, vmem),
        scratch_shapes=[
            pltpu.VMEM((FRAMES, HEADS * D, WIN), F32),
            pltpu.VMEM((FRAMES, HEADS * D, WIN), F32),
            pltpu.VMEM((STRIPS, FRAMES, CELLS, 256), F32),
            pltpu.VMEM((STRIPS, 2, CELLS, 256), F32),
            pltpu.VMEM((14, 32, 128), F32),
            pltpu.SemaphoreType.DMA((2, FRAMES)),
            pltpu.SemaphoreType.DMA((2,)),
        ],
        compiler_params=pltpu.CompilerParams(vmem_limit_bytes=VMEM_LIMIT),
        name="key_side",
    )(k, v, after, local, got, halo, tw)


def body(query_feat, key_feat, value_feat, grad_out, spatial_weight, temporal_weight):
    head = lax.axis_index("head")
    chans = HEADS * D
    w_own = lax.dynamic_slice_in_dim(spatial_weight.reshape(9, STRIPS * chans), head * chans, chans, axis=1)
    w_own = jnp.pad(w_own, ((0, 0), (0, 256 - chans)))
    tw = jnp.pad(jnp.transpose(temporal_weight.reshape(3, STRIPS, chans), (1, 0, 2)), ((0, 0), (0, 0), (0, 256 - chans)))
    local = key_value_sums(key_feat, value_feat)
    before = prefix(local[:, FRAMES - 1].reshape(4, 56, 128)).reshape(HEADS, D, 128)
    gq, later, act = query_side(query_feat, grad_out, before, local, w_own)
    got, halo, after = exchange(act, later[:, 0].reshape(4, 56, 128))
    gk, gv, mixed = key_side(key_feat, value_feat, after.reshape(HEADS, D, 128), later, got, halo, tw)
    mixed = jnp.transpose(mixed.reshape(ROWS, 5, FRAMES, STRIPS * chans), (2, 0, 1, 3))
    return gq, gk, gv, mixed


def solution(mesh):
    wide = P("head", "seg")
    in_specs = (wide, wide, wide, wide, P(), P())
    out_specs = (wide, wide, wide, P("seg", None, "head", None))
    return jax.shard_map(body, mesh=mesh, in_specs=in_specs, out_specs=out_specs, check_vma=False)
```

profile of v0, /device:TPU:2, one launch (start us, length us, event | category | flops | bytes accessed | tf_op | source)
XLA Modules:
  0.0 116.3 jit_solution(1662167722680831286)
XLA Ops:
  0.6 0.8 reshape.26
  1.5 0.6 pad.9.tw_ref
  2.1 0.9 reshape.24
  3.0 0.1 constant_dynamic-slice_fusion
  3.1 0.6 pad.8.w_ref
  3.7 4.8 %key_value_sums.1.local_ref = f32[2,4,112,128]{3,2,1,0:T(8,128)} custom-call(f32[224,3200]{1,0:T(8,128)} %k_ref.3, f32[224,3200]{1,0:T(8,128)} %v_ref.3), custom_call_target="tpu_custom_call" | custom-call | tf_op jit(solution)/shard_map/key_value_sums/pallas_call | solution.py:102
  8.6 1.6 %slice.8 = f32[2,1,112,128]{3,2,1,0:T(8,128)} slice(f32[2,4,112,128]{3,2,1,0:T(8,128)} %key_value_sums.1.local_ref), slice={[0:2], [3:4], [0:112], [0:128]} | slice | bytes 229376 | tf_op jit(solution)/shard_map/slice | solution.py:527
  10.1 16.8 %prefix.1 = f32[4,56,128]{2,1,0:T(8,128)} custom-call(f32[4,56,128]{2,1,0:T(8,128)} %bitcast.12), custom_call_target="tpu_custom_call" | custom-call | tf_op jit(solution)/shard_map/prefix/pallas_call | solution.py:217
  26.9 17.1 %query_side.1 = (f32[224,3200]{1,0:T(8,128)}, f32[2,4,112,128]{3,2,1,0:T(8,128)}, f32[4,8,100,256]{3,2,1,0:T(8,128)}) custom-call(f32[224,3200]{1,0:T(8,128)} %q_ref.1, f32[224,3200]{1,0:T(8,128)} %g_ref.1, f32[2,112,128]{2,1,0:T(8,128)} %bitcast.13, f32[2,4,112,128]{3,2,1,0:T(8,128)} %key_value_sums.1.local_ref, f32[9,256]{1,0:T(8,128)} %pad.8.w_ref), custom_call_target="tpu_custom_call" | custom-call | tf_op jit(solution)/shard_map/query_side/pallas_call | solution.py:306
  44.0 0.9 slice.7
  44.9 0.0 copy-start
  44.9 2.0 %copy-done = f32[4,8,100,256]{3,2,1,0:T(8,128)S(1)} copy-done((f32[4,8,100,256]{3,2,1,0:T(8,128)S(1)}, f32[4,8,100,256]{3,2,1,0:T(8,128)}, u32[]{:S(2)}) %copy-start) | copy-done | bytes 3276824
  46.9 54.9 %exchange.1 = (f32[8,4,100,256]{3,2,1,0:T(8,128)S(1)}, f32[8,2,100,256]{3,2,1,0:T(8,128)S(1)}, f32[4,56,128]{2,1,0:T(8,128)S(1)}) custom-call(f32[4,8,100,256]{3,2,1,0:T(8,128)S(1)} %copy-done, f32[4,56,128]{2,1,0:T(8,128)S(1)} %bitcast.10), custom_call_target="tpu_custom_call" | custom-call | tf_op jit(solution)/shard_map/exchange/pallas_call | solution.py:387
  101.8 0.0 copy-start.1
  101.8 1.7 %copy-done.1 = f32[8,4,100,256]{3,2,1,0:T(8,128)} copy-done((f32[8,4,100,256]{3,2,1,0:T(8,128)}, f32[8,4,100,256]{3,2,1,0:T(8,128)S(1)}, u32[]{:S(2)}) %copy-start.1) | copy-done | bytes 3276824
  103.5 0.0 copy-start.2
  103.6 1.2 %copy-done.2 = f32[8,2,100,256]{3,2,1,0:T(8,128)} copy-done((f32[8,2,100,256]{3,2,1,0:T(8,128)}, f32[8,2,100,256]{3,2,1,0:T(8,128)S(1)}, u32[]{:S(2)}) %copy-start.2) | copy-done | bytes 1638424
  104.8 0.0 copy-start.3
  104.8 0.6 copy-done.3
  105.4 10.9 %key_side.1 = (f32[224,3200]{1,0:T(8,128)}, f32[224,3200]{1,0:T(8,128)}, f32[100,4,1792]{2,1,0:T(4,128)}) custom-call(f32[224,3200]{1,0:T(8,128)} %k_ref.3, f32[224,3200]{1,0:T(8,128)} %v_ref.3, f32[2,112,128]{2,1,0:T(8,128)} %bitcast.11, f32[2,4,112,128]{3,2,1,0:T(8,128)} %get-tuple-element.15.local_ref, f32[8,4,100,256]{3,2,1,0:T(8,128)} %copy-done.1, ...), custom_call_target="tpu_custom_call" | custom-call | tf_op jit(solution)/shard_map/key_side/pallas_call | solution.py:497
  (1 shorter events, 0.0 us)
Async XLA Ops:
  44.9 2.0 %copy-start = (f32[4,8,100,256]{3,2,1,0:T(8,128)S(1)}, f32[4,8,100,256]{3,2,1,0:T(8,128)}, u32[]{:S(2)}) copy-start(f32[4,8,100,256]{3,2,1,0:T(8,128)} %get-tuple-element.14.act_ref) | copy-start | bytes 9830404
  101.8 1.7 %copy-start.1 = (f32[8,4,100,256]{3,2,1,0:T(8,128)}, f32[8,4,100,256]{3,2,1,0:T(8,128)S(1)}, u32[]{:S(2)}) copy-start(f32[8,4,100,256]{3,2,1,0:T(8,128)S(1)} %get-tuple-element.17.got_hbm) | copy-start | bytes 9830404
  103.5 1.2 %copy-start.2 = (f32[8,2,100,256]{3,2,1,0:T(8,128)}, f32[8,2,100,256]{3,2,1,0:T(8,128)S(1)}, u32[]{:S(2)}) copy-start(f32[8,2,100,256]{3,2,1,0:T(8,128)S(1)} %get-tuple-element.18.halo_hbm) | copy-start | bytes 4915204
  104.8 0.7 copy-start.3
where the time goes:
time: 117 us; the launch traced here: 116 us
  Pallas kernels  104 us (89%)
  local copies, waits for them, and re-layouts  11.1 us (9%)
    pallas_call x1, Pallas kernels, exchange(): pl.pallas_call(exchange_kernel, out_shape=(jax.ShapeDtypeStruct((STRIPS,...  54.9 us
    pallas_call x1, Pallas kernels, query_side(): pl.pallas_call(query_kernel, out_shape=(jax.ShapeDtypeStruct((HEADS * D,...  17.1 us
    pallas_call x1, Pallas kernels, prefix(): pl.pallas_call(scan_kernel, out_shape=jax.ShapeDtypeStruct((4, 56, 128),...  16.8 us
    pallas_call x1, Pallas kernels, key_side(): pl.pallas_call(key_kernel, out_shape=(jax.ShapeDtypeStruct((HEADS * D, 32...  10.9 us
    unnamed x8, local copies, waits for them, and re-layouts  5.55 us
    pallas_call x1, Pallas kernels, key_value_sums(): pl.pallas_call(sums_kernel, out_shape=jax.ShapeDtypeStruct((HEADS, FRAMES...  4.82 us

commit v1 on v0

v1 whole, which is shorter than its diff:
```python
import functools

import jax
import jax.numpy as jnp
from jax import lax
from jax.experimental import pallas as pl
from jax.experimental.pallas import tpu as pltpu
from jax.sharding import PartitionSpec as P

D = 112
ROWS = 20
COLS = 40
FRAMES = 4
STRIDE = 768
WIN = 896
HEADS = 2
STRIPS = 8
CELLS = 100
CHUNKS = ((0, 256), (256, 256), (512, 256), (768, 128))
BASE = 136
MESH = pl.DeviceIdType.MESH
F32 = jnp.float32
BF16 = jnp.bfloat16
VMEM_LIMIT = 60 * 1024 * 1024


def split(x):
    hi = x.astype(BF16)
    lo = (x - hi.astype(F32)).astype(BF16)
    return hi, lo


def nn(a, b):
    return lax.dot_general(a, b, (((1,), (0,)), ((), ())), preferred_element_type=F32)


def nt(a, b):
    return lax.dot_general(a, b, (((1,), (1,)), ((), ())), preferred_element_type=F32)


def pad_rows(x):
    return jnp.concatenate([x, jnp.zeros((16, x.shape[1]), x.dtype)], axis=0)


def left_mul(pair, b_hi, b_lo):
    return nn(pair, jnp.concatenate([b_hi, b_hi], axis=0)) + nn(pair[:, :128], b_lo)


def outer(a_hi, a_lo, b_hi, b_lo):
    both = nt(jnp.concatenate([a_hi, a_lo], axis=0), b_hi)
    rows = a_hi.shape[0]
    return both[:rows] + both[rows:] + nt(a_hi, b_lo)


def in_frame(frame, start, width):
    lane = lax.broadcasted_iota(jnp.int32, (1, width), 1) + start
    return (lane >= 32 * frame) & (lane < 32 * frame + ROWS * COLS)


def extra_row(row):
    place = lax.broadcasted_iota(jnp.int32, (16, row.shape[1]), 0)
    return jnp.where(place == 0, jnp.broadcast_to(row, (16, row.shape[1])), 0.0)


def side_by_side(x):
    hi, lo = split(x)
    return jnp.concatenate([hi, lo], axis=1)


def greet(devices):
    barrier = pltpu.get_barrier_semaphore()
    for dev in devices:
        pl.semaphore_signal(barrier, inc=1, device_id=dev, device_id_type=MESH)
    pl.semaphore_wait(barrier, len(devices))


def scan_peers():
    seg, head = lax.axis_index("seg"), lax.axis_index("head")
    x, y = seg // 4, seg % 4
    along_y = [(x * 4 + (y + k) % 4, head) for k in range(1, 4)]
    along_x = [(((x + k) % 4) * 4 + y, head) for k in range(1, 4)]
    return along_y, along_x


SCAN_SCRATCH = [
    pltpu.VMEM((4, 56, 128), F32),
    pltpu.VMEM((56, 128), F32),
    pltpu.VMEM((4, 56, 128), F32),
    pltpu.VMEM((4, 56, 128), F32),
    pltpu.SemaphoreType.DMA((3, 4)),
    pltpu.SemaphoreType.DMA((3, 4)),
]


class Scan:
    def __init__(self, own, result, scratch, reverse):
        self.own, self.result, self.reverse = own, result, reverse
        self.got, self.line, self.lines, self.back, self.send, self.recv = scratch
        seg = lax.axis_index("seg")
        self.x, self.y = seg // 4, seg % 4
        self.along_y, self.along_x = scan_peers()

    def copy(self, phase, k, src, dst, dev):
        return pltpu.make_async_remote_copy(
            src_ref=src, dst_ref=dst, send_sem=self.send.at[phase, k], recv_sem=self.recv.at[phase, k],
            device_id=dev, device_id_type=MESH,
        )

    def first(self):
        self.c1 = [
            self.copy(0, k, self.own.at[(self.y + k) % 4], self.got.at[k], self.along_y[k - 1])
            for k in range(1, 4)
        ]
        for c in self.c1:
            c.start()

    def second(self):
        for c in self.c1:
            c.wait()
        mine = self.own[self.y]
        self.line[...] = mine + self.got[1] + self.got[2] + self.got[3]
        self.c2 = [
            self.copy(1, k, self.line, self.lines.at[k], self.along_x[k - 1]) for k in range(1, 4)
        ]
        for c in self.c2:
            c.start()

    def counts(self, place, source):
        return source > place if self.reverse else source < place

    def third(self):
        for c in self.c2:
            c.wait()
        zero = jnp.zeros((56, 128), F32)
        before = zero
        for k in range(1, 4):
            source = (self.x + 4 - k) % 4
            before = before + jnp.where(self.counts(self.x, source), self.lines[k], zero)
        terms = [(self.y, self.own[self.y])] + [((self.y + 4 - k) % 4, self.got[k]) for k in range(1, 4)]
        for k in range(4):
            target = (self.y + k) % 4
            total = before
            for source, value in terms:
                total = total + jnp.where(self.counts(target, source), value, zero)
            self.back[k] = total
        self.c3 = [
            self.copy(2, k, self.back.at[k], self.result.at[self.y], self.along_y[k - 1]) for k in range(1, 4)
        ]
        for c in self.c3:
            c.start()
        self.result[self.y] = self.back[0]

    def last(self):
        for c in self.c3:
            c.wait()


def ones_row(width):
    return extra_row(jnp.ones((1, width), F32)).astype(BF16)


def sums_frame(h, f, k_win, v_win):
    rows = slice(D * h, D * h + D)
    total = jnp.zeros((D, 128), F32)
    for start, width in CHUNKS:
        lanes = slice(start, start + width)
        ok = in_frame(f, start, width)
        k_hi, k_lo = split(jnp.where(ok, jnp.exp(k_win[f, rows, lanes]), 0.0))
        v_hi, v_lo = split(v_win[f, rows, lanes])
        v_hi = jnp.concatenate([v_hi, ones_row(width)], axis=0)
        total = total + outer(k_hi, k_lo, v_hi, pad_rows(v_lo))
    return total


def rows_of(ref, h):
    return jnp.concatenate([ref[2 * h], ref[2 * h + 1]], axis=0)


def attend(f, q_win, state, att, inv):
    for h in range(HEADS):
        turned = side_by_side(pad_rows(state(h, f)).T)
        rows = slice(D * h, D * h + D)
        for start, width in CHUNKS:
            lanes = slice(start, start + width)
            q_hi, q_lo = split(jnp.exp(q_win[f, rows, lanes]))
            numer = left_mul(turned, pad_rows(q_hi), pad_rows(q_lo))
            inverse = 1.0 / numer[D:D + 1]
            att[f, rows, lanes] = jnp.where(in_frame(f, start, width), numer[:D] * inverse, 0.0)
            inv[f, h, 0:1, lanes] = inverse


def convolve(f, att, conv_in, w_own, send):
    for m in range(WIN // 128):
        place = BASE - 32 * f + 128 * m
        conv_in[place:place + 128, :] = att[f, :, 128 * m:128 * m + 128].T
    edge = lax.broadcasted_iota(jnp.int32, (COLS, 128), 0)
    for lane in range(2):
        lanes = slice(128 * lane, 128 * lane + 128)
        taps = [[w_own[i, j:j + 1, lanes] for j in range(3)] for i in range(3)]
        for r in range(ROWS):
            lines = [conv_in[BASE + COLS * (r + i - 1):BASE + COLS * (r + i), lanes] for i in range(3)]
            cols = [taps[0][j] * lines[0] + taps[1][j] * lines[1] + taps[2][j] * lines[2] for j in range(3)]
            total = (
                cols[1]
                + jnp.where(edge == 0, 0.0, pltpu.roll(cols[0], 1, 0))
                + jnp.where(edge == COLS - 1, 0.0, pltpu.roll(cols[2], COLS - 1, 0))
            )
            half = 0.5 * total
            act = half + half * jnp.tanh(half)
            for j in range(STRIPS):
                send[f, j, 5 * r:5 * r + 5, lanes] = act[5 * j:5 * j + 5]


def place_of(f, start, width):
    return slice(STRIDE * f + start, STRIDE * f + start + width)


def query_grads(f, q_win, g_win, state, att, inv, gq_ref, ds):
    for h in range(HEADS):
        plain = side_by_side(state(h, f))
        rows = slice(D * h, D * h + D)
        grad_state = jnp.zeros((D, 128), F32)
        for start, width in CHUNKS:
            lanes = slice(start, start + width)
            ok = in_frame(f, start, width)
            feat = jnp.exp(q_win[f, rows, lanes])
            q_hi, q_lo = split(feat)
            inverse = inv[f, h, 0:1, lanes]
            grad = g_win[f, rows, lanes]
            slope = -jnp.sum(grad * att[f, rows, lanes], axis=0, keepdims=True) * inverse
            ext = jnp.where(ok, jnp.concatenate([grad * inverse, extra_row(slope)], axis=0), 0.0)
            n_hi, n_lo = split(ext)
            gq = left_mul(plain, n_hi, n_lo) * feat
            place = place_of(f, start, width)
            gq_ref[rows, place] = jnp.where(ok, gq, gq_ref[rows, place])
            grad_state = grad_state + outer(q_hi, q_lo, n_hi, n_lo)
        ds[h, f] = grad_state


def key_grads(f, k_win, v_win, state, gk_ref, gv_ref):
    for h in range(HEADS):
        plain = side_by_side(state(h, f))
        turned = side_by_side(pad_rows(state(h, f)).T)
        rows = slice(D * h, D * h + D)
        for start, width in CHUNKS:
            lanes = slice(start, start + width)
            ok = in_frame(f, start, width)
            feat = jnp.exp(k_win[f, rows, lanes])
            k_hi, k_lo = split(feat)
            v_hi, v_lo = split(v_win[f, rows, lanes])
            v_hi = jnp.concatenate([v_hi, ones_row(width)], axis=0)
            gk = left_mul(plain, v_hi, pad_rows(v_lo)) * feat
            gv = left_mul(turned, pad_rows(k_hi), pad_rows(k_lo))[:D]
            place = place_of(f, start, width)
            gk_ref[rows, place] = jnp.where(ok, gk, gk_ref[rows, place])
            gv_ref[rows, place] = jnp.where(ok, gv, gv_ref[rows, place])


ORDER = (2, 3, 0, 1)
HOPS = (1, 2, 6, 3, 5, 7, 4)


def main_kernel(q_ref, k_ref, v_ref, g_ref, sw_ref, gq_ref, gk_ref, gv_ref, got_ref, halo_ref,
                q_win, k_win, v_win, g_win, att, inv, conv_in, act, w_own, local, ds, own, before, after,
                load, send, recv, fsend, frecv, lsem, *scratch):
    seg, head = lax.axis_index("seg"), lax.axis_index("head")
    along_y, along_x = scan_peers()
    peers = [(seg, head ^ k) for k in range(1, 8)]
    up, down = ((seg + 1) % 16, head), ((seg + 15) % 16, head)
    barrier = pltpu.get_barrier_semaphore()
    for dev in along_y + along_x + peers + [up, down]:
        pl.semaphore_signal(barrier, inc=1, device_id=dev, device_id_type=MESH)

    wins = ((k_ref, k_win), (v_ref, v_win), (q_ref, q_win), (g_ref, g_win))

    def loading(i, f):
        src, dst = wins[i]
        return pltpu.make_async_copy(src.at[:, STRIDE * f:STRIDE * f + WIN], dst.at[f], load.at[i, f])

    for f in range(FRAMES):
        for i in range(2):
            loading(i, f).start()
    for i in (2, 3):
        for f in ORDER:
            loading(i, f).start()

    def strip(f, k):
        return pltpu.make_async_remote_copy(
            src_ref=act.at[f, head ^ k], dst_ref=got_ref.at[k, f], send_sem=send.at[f, k], recv_sem=recv.at[f, k],
            device_id=(seg, head ^ k), device_id_type=MESH,
        )

    def forward(f, k):
        src = act.at[f, head] if k == 0 else got_ref.at[k, f]
        return pltpu.make_async_remote_copy(
            src_ref=src, dst_ref=halo_ref.at[k, f - 2], send_sem=fsend.at[f - 2, k], recv_sem=frecv.at[f - 2, k],
            device_id=up, device_id_type=MESH,
        )

    def mine(f):
        return pltpu.make_async_copy(act.at[f, head], got_ref.at[0, f], lsem.at[f])

    queue = [(2, 0), (3, 0), (2, 1), (3, 1)] + [(2, k) for k in HOPS[1:]] + [(3, k) for k in HOPS[1:]]

    def pass_on(count):
        for f, k in queue[:count]:
            if k:
                strip(f, k).wait_recv()
            forward(f, k).start()
        del queue[:count]

    lanes = pl.ds(0, 256)
    chans = HEADS * D
    for i in range(3):
        taps = sw_ref[i, :, :256]
        for o in range(1, STRIPS):
            begin = min(chans * o, STRIPS * chans - 256)
            part = sw_ref[i, :, begin:begin + 256]
            if begin < chans * o:
                part = pltpu.roll(part, 256 - (chans * o - begin), 1)
            taps = jnp.where(head == o, part, taps)
        w_own[i, 0:3] = taps
    att[...] = jnp.zeros_like(att)
    conv_in[...] = jnp.zeros_like(conv_in)

    for f in range(FRAMES):
        loading(0, f).wait()
        loading(1, f).wait()
        for h in range(HEADS):
            local[h, f] = sums_frame(h, f, k_win, v_win)
    for h in range(HEADS):
        for f in range(1, FRAMES):
            local[h, f] = local[h, f] + local[h, f - 1]
        own[2 * h], own[2 * h + 1] = local[h, FRAMES - 1, :56], local[h, FRAMES - 1, 56:]
    pl.semaphore_wait(barrier, 15)
    scan = Scan(own, before, scratch[:6], False)
    scan.first()
    scan.second()
    scan.third()
    scan.last()

    def state(h, f):
        return rows_of(before, h) + local[h, f]

    for i, f in enumerate(ORDER):
        loading(2, f).wait()
        attend(f, q_win, state, att, inv)
        convolve(f, att, conv_in, w_own, act)
        for k in HOPS:
            strip(f, k).start()
        mine(f).start()
        pass_on((1, 2, 2, 2)[i])
    for i, f in enumerate(ORDER):
        loading(3, f).wait()
        query_grads(f, q_win, g_win, state, att, inv, gq_ref, ds)
        pass_on((1, 0, 1, 0)[i])
    for h in range(HEADS):
        for f in range(FRAMES - 2, -1, -1):
            ds[h, f] = ds[h, f] + ds[h, f + 1]
        own[2 * h], own[2 * h + 1] = ds[h, 0, :56], ds[h, 0, 56:]
    scan = Scan(own, after, scratch[6:], True)
    scan.first()
    pass_on(1)
    scan.second()
    pass_on(2)
    scan.third()
    pass_on(1)
    scan.last()
    pass_on(len(queue))

    def later(h, f):
        return rows_of(after, h) + ds[h, f]

    for f in range(FRAMES):
        key_grads(f, k_win, v_win, later, gk_ref, gv_ref)
    for f in range(FRAMES):
        mine(f).wait()
    for f in (0, 1):
        for k in HOPS:
            strip(f, k).wait_recv()
    for f in ORDER:
        for k in HOPS:
            strip(f, k).wait_send()
    for f in (2, 3):
        for k in (0,) + HOPS:
            forward(f, k).wait()


def main_call(q, k, v, g, weights):
    hbm = pl.BlockSpec(memory_space=pl.ANY)
    vmem = pl.BlockSpec(memory_space=pltpu.VMEM)
    wide = jax.ShapeDtypeStruct((HEADS * D, STRIDE * 3 + WIN), F32)
    window = pltpu.VMEM((FRAMES, HEADS * D, WIN), F32)
    states = pltpu.VMEM((HEADS, FRAMES, D, 128), F32)
    quarters = pltpu.VMEM((4, 56, 128), F32)
    return pl.pallas_call(
        main_kernel,
        out_shape=(
            wide,
            wide,
            wide,
            jax.ShapeDtypeStruct((STRIPS, FRAMES, CELLS, 256), F32),
            jax.ShapeDtypeStruct((STRIPS, 2, CELLS, 256), F32),
        ),
        in_specs=[hbm] * 4 + [vmem],
        out_specs=(vmem, vmem, vmem, hbm, hbm),
        scratch_shapes=[
            window, window, window, window,
            pltpu.VMEM((FRAMES, 256, WIN), F32),
            pltpu.VMEM((FRAMES, HEADS, 8, WIN), F32),
            pltpu.VMEM((BASE + WIN, 256), F32),
            pltpu.VMEM((FRAMES, STRIPS, CELLS, 256), F32),
            pltpu.VMEM((3, 8, 256), F32),
            states, states, quarters, quarters, quarters,
            pltpu.SemaphoreType.DMA((4, FRAMES)),
            pltpu.SemaphoreType.DMA((FRAMES, 8)),
            pltpu.SemaphoreType.DMA((FRAMES, 8)),
            pltpu.SemaphoreType.DMA((2, 8)),
            pltpu.SemaphoreType.DMA((2, 8)),
            pltpu.SemaphoreType.DMA((FRAMES,)),
        ] + SCAN_SCRATCH + SCAN_SCRATCH,
        compiler_params=pltpu.CompilerParams(collective_id=0, has_side_effects=True, vmem_limit_bytes=46 << 20),
        name="attention_exchange",
    )(q, k, v, g, weights)


def mix_group(base, count, halo_on, got, halo, tw_ref, tmp, mixed_ref):
    head = lax.axis_index("head")
    place = lax.broadcasted_iota(jnp.int32, (count, 128), 1)
    pending = [None] * FRAMES
    for owner in range(STRIPS):
        slot = head ^ owner
        for lane in range(2):
            lanes = slice(128 * lane, 128 * lane + 128)
            acts = [jnp.where(halo_on, halo[slot, i, pl.ds(base, count), lanes], 0.0) for i in range(2)]
            acts += [got[slot, f, pl.ds(base, count), lanes] for f in range(FRAMES)]
            w = [tw_ref[owner, i:i + 1, lanes] for i in range(3)]
            width = 128 if lane == 0 else 96
            tile, shift = divmod(224 * owner + 128 * lane, 128)
            for f in range(FRAMES):
                val = w[0] * acts[f + 2] + w[1] * acts[f + 1] + w[2] * acts[f]
                full = val
                if shift:
                    val = pltpu.roll(val, shift, 1)
                    full = jnp.where(place < shift, pending[f], val)
                if shift + width >= 128:
                    tmp[tile, pl.ds(f, count, stride=4), :] = full
                    pending[f] = val
                else:
                    pending[f] = full


def mix_kernel(got, halo, tw_ref, mixed_ref, tmp, tw):
    for owner in range(STRIPS):
        begin = min(224 * owner, 1792 - 256)
        part = tw_ref[:, begin:begin + 256]
        if begin < 224 * owner:
            part = pltpu.roll(part, 256 - (224 * owner - begin), 1)
        tw[owner, 0:3] = part
    halo_on = lax.axis_index("seg") > 0

    def group(base, count):
        mix_group(base, count, halo_on, got, halo, tw, tmp, mixed_ref)
        for i in range(count):
            for t in range(14):
                mixed_ref[base + i, :, 128 * t:128 * t + 128] = tmp[t, 4 * i:4 * i + 4, :]

    def step(i, carry):
        group(pl.multiple_of(8 * i, 8), 8)
        return carry

    lax.fori_loop(0, 12, step, 0)
    group(96, 4)


def mix(got, halo, tw):
    vmem = pl.BlockSpec(memory_space=pltpu.VMEM)
    return pl.pallas_call(
        mix_kernel,
        out_shape=jax.ShapeDtypeStruct((CELLS, FRAMES, 1792), F32),
        in_specs=[vmem] * 3,
        out_specs=vmem,
        scratch_shapes=[pltpu.VMEM((14, 32, 128), F32), pltpu.VMEM((STRIPS, 8, 256), F32)],
        compiler_params=pltpu.CompilerParams(vmem_limit_bytes=24 << 20),
        name="mix",
    )(got, halo, tw)


def body(query_feat, key_feat, value_feat, grad_out, spatial_weight, temporal_weight):
    gq, gk, gv, got, halo = main_call(query_feat, key_feat, value_feat, grad_out, spatial_weight)
    mixed = mix(got, halo, temporal_weight)
    mixed = jnp.transpose(mixed.reshape(ROWS, 5, FRAMES, STRIPS * HEADS * D), (2, 0, 1, 3))
    return gq, gk, gv, mixed


def solution(mesh):
    wide = P("head", "seg")
    in_specs = (wide, wide, wide, wide, P(), P())
    out_specs = (wide, wide, wide, P("seg", None, "head", None))
    return jax.shard_map(body, mesh=mesh, in_specs=in_specs, out_specs=out_specs, check_vma=False)
```

time: 117 us -> 79.8 us (0.68)
  Pallas kernels: 104 us -> 69 us
  local copies, waits for them, and re-layouts: 11.1 us -> 8.83 us
    pallas_call x5 -> x2, Pallas kernels: 104 us -> 69 us  [the longest x1 65.5 us: main_call(): pl.pallas_call(main_kernel, out_shape=(wide, wide, wide, jax.ShapeDtypeSt...]
    unnamed x8 -> x11, local copies, waits for them, and re-layouts: 5.55 us -> 8.83 us
    slice x2 -> x0, local copies, waits for them, and re-layouts: 2.47 us -> none  [the longest x1 1.56 us: body(): local[:, FRAMES - 1].reshape(4, 56, 128)]
    reshape x3 -> x0, local copies, waits for them, and re-layouts: 1.77 us -> none  [the longest x1 0.92 us: body(): spatial_weight.reshape(9, STRIPS * chans)]
    pad x2 -> x0, local copies, waits for them, and re-layouts: 1.23 us -> none  [the longest x1 0.62 us: body(): jnp.pad(jnp.transpose(temporal_weight.reshape(3, STRIPS, chans), (1, 0, 2...]
where the time goes in v1:
time: 79.8 us; the launch traced here: 78.5 us
  Pallas kernels  69 us (86%)
  local copies, waits for them, and re-layouts  8.83 us (11%)
    pallas_call x1, Pallas kernels, main_call(): pl.pallas_call(main_kernel, out_shape=(wide, wide, wide, jax.ShapeDtypeSt...  65.5 us
    unnamed x11, local copies, waits for them, and re-layouts  8.83 us
    pallas_call x1, Pallas kernels, mix(): pl.pallas_call(mix_kernel, out_shape=jax.ShapeDtypeStruct((CELLS, FRAMES,...  3.52 us

profile of v1, /device:TPU:2, one launch (start us, length us, event | category | flops | bytes accessed | tf_op | source)
XLA Modules:
  0.0 78.5 jit_solution(3440977999693383739)
XLA Ops:
  0.6 0.0 copy-start.1
  0.6 0.9 %copy-done.1 = f32[3,3,1792]{2,1,0:T(4,128)S(1)} copy-done((f32[3,3,1792]{2,1,0:T(4,128)S(1)}, f32[3,3,1792]{2,1,0:T(4,128)}, u32[]{:S(2)}) %copy-start.1) | copy-done | bytes 64536
  1.5 0.0 copy-start.2
  1.5 65.5 %attention_exchange.1 = (f32[224,3200]{1,0:T(8,128)S(1)}, f32[224,3200]{1,0:T(8,128)S(1)}, f32[224,3200]{1,0:T(8,128)}, f32[8,4,100,256]{3,2,1,0:T(8,128)}, f32[8,2,100,256]{3,2,1,0:T(8,128)S(1)}) custom-call(f32[224,3200]{1,0:T(8,128)} %q_ref.1, f32[224,3200]{1,0:T(8,128)} %k_ref.1, f32[224,3200]{1,0:T(8,128)} %v_ref.1, f32[224,3200]{1,0:T(8,128)} %g_ref.1, ...), custom_call_target="tpu_custom_call" | custom-call | tf_op jit(solution)/shard_map/attention_exchange/pallas_call | solution.py:396
  67.0 0.0 copy-done.2
  67.0 0.0 copy-start
  67.0 2.0 %copy-done = f32[8,4,100,256]{3,2,1,0:T(8,128)S(1)} copy-done((f32[8,4,100,256]{3,2,1,0:T(8,128)S(1)}, f32[8,4,100,256]{3,2,1,0:T(8,128)}, u32[]{:S(2)}) %copy-start) | copy-done | bytes 3276824
  69.0 3.5 %mix.1 = f32[100,4,1792]{2,1,0:T(4,128)} custom-call(f32[8,4,100,256]{3,2,1,0:T(8,128)S(1)} %copy-done, f32[8,2,100,256]{3,2,1,0:T(8,128)S(1)} %get-tuple-element.13.halo, f32[3,1792]{1,0:T(4,128)S(1)} %copy-done.2), custom_call_target="tpu_custom_call" | custom-call | tf_op jit(solution)/shard_map/mix/pallas_call | solution.py:478
  72.5 1.6 %copy.13 = f32[224,3200]{1,0:T(8,128)} copy(f32[224,3200]{1,0:T(8,128)S(1)} %get-tuple-element.18) | data formatting | bytes 5734400
  74.1 0.0 copy-start.3
  74.1 1.6 %copy.14 = f32[224,3200]{1,0:T(8,128)} copy(f32[224,3200]{1,0:T(8,128)S(1)} %get-tuple-element.19) | data formatting | bytes 5734400
  75.6 1.3 %copy-done.3 = f32[224,3200]{1,0:T(8,128)S(1)} copy-done((f32[224,3200]{1,0:T(8,128)S(1)}, f32[224,3200]{1,0:T(8,128)}, u32[]{:S(2)}) %copy-start.3) | copy-done | bytes 2867224
  76.9 1.6 %copy.15 = f32[224,3200]{1,0:T(8,128)} copy(f32[224,3200]{1,0:T(8,128)S(1)} %copy-done.3) | data formatting | bytes 5734400
Async XLA Ops:
  0.6 0.9 %copy-start.1 = (f32[3,3,1792]{2,1,0:T(4,128)S(1)}, f32[3,3,1792]{2,1,0:T(4,128)}, u32[]{:S(2)}) copy-start(f32[3,3,1792]{2,1,0:T(4,128)} %sw_ref.1) | copy-start | bytes 193540
  1.5 65.5 %copy-start.2 = (f32[3,1792]{1,0:T(4,128)S(1)}, f32[3,1792]{1,0:T(4,128)}, u32[]{:S(2)}) copy-start(f32[3,1792]{1,0:T(4,128)} %tw_ref.1) | copy-start | bytes 64516
  67.0 2.0 %copy-start = (f32[8,4,100,256]{3,2,1,0:T(8,128)S(1)}, f32[8,4,100,256]{3,2,1,0:T(8,128)}, u32[]{:S(2)}) copy-start(f32[8,4,100,256]{3,2,1,0:T(8,128)} %get-tuple-element.12.got) | copy-start | bytes 9830404
  74.1 2.8 %copy-start.3 = (f32[224,3200]{1,0:T(8,128)S(1)}, f32[224,3200]{1,0:T(8,128)}, u32[]{:S(2)}) copy-start(f32[224,3200]{1,0:T(8,128)} %get-tuple-element.20) | copy-start | bytes 8601604

commit v2 on v1

--- a/solution.py
+++ b/solution.py
@@ -16,12 +16,15 @@
 HEADS = 2
 STRIPS = 8
 CELLS = 100
+SPLIT = 80
+PACKED = SPLIT + CELLS
 CHUNKS = ((0, 256), (256, 256), (512, 256), (768, 128))
 BASE = 136
 MESH = pl.DeviceIdType.MESH
 F32 = jnp.float32
 BF16 = jnp.bfloat16
-VMEM_LIMIT = 60 * 1024 * 1024
+MAIN_LIMIT = 43 << 20
+MIX_LIMIT = 43 << 20
 
 
 def split(x):
@@ -74,84 +77,59 @@
     pl.semaphore_wait(barrier, len(devices))
 
 
-def scan_peers():
+SEGS = 16
+PIECE = 16
+SCAN_SCRATCH = [
+    pltpu.VMEM((SEGS, PIECE, 128), F32),
+    pltpu.VMEM((SEGS, PIECE, 128), F32),
+    pltpu.SemaphoreType.DMA((2, SEGS)),
+    pltpu.SemaphoreType.DMA((2, SEGS)),
+]
+
+
+def seg_peers():
     seg, head = lax.axis_index("seg"), lax.axis_index("head")
-    x, y = seg // 4, seg % 4
-    along_y = [(x * 4 + (y + k) % 4, head) for k in range(1, 4)]
-    along_x = [(((x + k) % 4) * 4 + y, head) for k in range(1, 4)]
-    return along_y, along_x
-
-
-SCAN_SCRATCH = [
-    pltpu.VMEM((4, 56, 128), F32),
-    pltpu.VMEM((56, 128), F32),
-    pltpu.VMEM((4, 56, 128), F32),
-    pltpu.VMEM((4, 56, 128), F32),
-    pltpu.SemaphoreType.DMA((3, 4)),
-    pltpu.SemaphoreType.DMA((3, 4)),
-]
+    return [((seg + k) % SEGS, head) for k in range(1, SEGS)]
 
 
 class Scan:
     def __init__(self, own, result, scratch, reverse):
         self.own, self.result, self.reverse = own, result, reverse
-        self.got, self.line, self.lines, self.back, self.send, self.recv = scratch
-        seg = lax.axis_index("seg")
-        self.x, self.y = seg // 4, seg % 4
-        self.along_y, self.along_x = scan_peers()
-
-    def copy(self, phase, k, src, dst, dev):
+        self.got, self.back, self.send, self.recv = scratch
+        self.seg = lax.axis_index("seg")
+        self.peers = seg_peers()
+
+    def copy(self, phase, k, src, dst):
         return pltpu.make_async_remote_copy(
             src_ref=src, dst_ref=dst, send_sem=self.send.at[phase, k], recv_sem=self.recv.at[phase, k],
-            device_id=dev, device_id_type=MESH,
+            device_id=self.peers[k - 1], device_id_type=MESH,
         )
 
     def first(self):
         self.c1 = [
-            self.copy(0, k, self.own.at[(self.y + k) % 4], self.got.at[k], self.along_y[k - 1])
-            for k in range(1, 4)
+            self.copy(0, k, self.own.at[(self.seg + k) % SEGS], self.got.at[self.seg]) for k in range(1, SEGS)
         ]
         for c in self.c1:
             c.start()
+        self.got[self.seg] = self.own[self.seg]
 
     def second(self):
         for c in self.c1:
             c.wait()
-        mine = self.own[self.y]
-        self.line[...] = mine + self.got[1] + self.got[2] + self.got[3]
+        total = jnp.zeros((PIECE, 128), F32)
+        order = range(SEGS - 1, -1, -1) if self.reverse else range(SEGS)
+        for j in order:
+            self.back[j] = total
+            total = total + self.got[j]
         self.c2 = [
-            self.copy(1, k, self.line, self.lines.at[k], self.along_x[k - 1]) for k in range(1, 4)
+            self.copy(1, k, self.back.at[(self.seg + k) % SEGS], self.result.at[self.seg]) for k in range(1, SEGS)
         ]
         for c in self.c2:
             c.start()
-
-    def counts(self, place, source):
-        return source > place if self.reverse else source < place
-
-    def third(self):
+        self.result[self.seg] = self.back[self.seg]
+
+    def last(self):
         for c in self.c2:
-            c.wait()
-        zero = jnp.zeros((56, 128), F32)
-        before = zero
-        for k in range(1, 4):
-            source = (self.x + 4 - k) % 4
-            before = before + jnp.where(self.counts(self.x, source), self.lines[k], zero)
-        terms = [(self.y, self.own[self.y])] + [((self.y + 4 - k) % 4, self.got[k]) for k in range(1, 4)]
-        for k in range(4):
-            target = (self.y + k) % 4
-            total = before
-            for source, value in terms:
-                total = total + jnp.where(self.counts(target, source), value, zero)
-            self.back[k] = total
-        self.c3 = [
-            self.copy(2, k, self.back.at[k], self.result.at[self.y], self.along_y[k - 1]) for k in range(1, 4)
-        ]
-        for c in self.c3:
-            c.start()
-        self.result[self.y] = self.back[0]
-
-    def last(self):
-        for c in self.c3:
             c.wait()
 
 
@@ -173,7 +151,12 @@
 
 
 def rows_of(ref, h):
-    return jnp.concatenate([ref[2 * h], ref[2 * h + 1]], axis=0)
+    return jnp.concatenate([ref[7 * h + i] for i in range(7)], axis=0)
+
+
+def put_rows(ref, h, value):
+    for i in range(7):
+        ref[7 * h + i] = value[PIECE * i:PIECE * i + PIECE]
 
 
 def attend(f, q_win, state, att, inv):
@@ -189,7 +172,7 @@
             inv[f, h, 0:1, lanes] = inverse
 
 
-def convolve(f, att, conv_in, w_own, send):
+def convolve(f, att, conv_in, w_own, send, rest):
     for m in range(WIN // 128):
         place = BASE - 32 * f + 128 * m
         conv_in[place:place + 128, :] = att[f, :, 128 * m:128 * m + 128].T
@@ -208,7 +191,18 @@
             half = 0.5 * total
             act = half + half * jnp.tanh(half)
             for j in range(STRIPS):
-                send[f, j, 5 * r:5 * r + 5, lanes] = act[5 * j:5 * j + 5]
+                part = act[5 * j:5 * j + 5]
+                if lane == 0:
+                    send[f, j, SPLIT + 5 * r:SPLIT + 5 * r + 5, :] = part
+                elif 5 * r < SPLIT:
+                    send[f, j, 5 * r:5 * r + 5, :] = part
+                else:
+                    rest[j, 5 * r - SPLIT:5 * r - SPLIT + 5, :] = part
+    free = lax.broadcasted_iota(jnp.int32, (24, 128), 1) >= 96
+    for j in range(STRIPS):
+        for p in range(3):
+            rows = slice(24 * p, 24 * p + 24)
+            send[f, j, rows, :] = jnp.where(free, pltpu.roll(rest[j], 96 - 32 * p, 1), send[f, j, rows, :])
 
 
 def place_of(f, start, width):
@@ -261,14 +255,13 @@
 
 
 def main_kernel(q_ref, k_ref, v_ref, g_ref, sw_ref, gq_ref, gk_ref, gv_ref, got_ref, halo_ref,
-                q_win, k_win, v_win, g_win, att, inv, conv_in, act, w_own, local, ds, own, before, after,
+                q_win, k_win, v_win, g_win, att, inv, conv_in, act, rest, w_own, local, ds, own, before, after,
                 load, send, recv, fsend, frecv, lsem, *scratch):
     seg, head = lax.axis_index("seg"), lax.axis_index("head")
-    along_y, along_x = scan_peers()
     peers = [(seg, head ^ k) for k in range(1, 8)]
-    up, down = ((seg + 1) % 16, head), ((seg + 15) % 16, head)
+    up = ((seg + 1) % SEGS, head)
     barrier = pltpu.get_barrier_semaphore()
-    for dev in along_y + along_x + peers + [up, down]:
+    for dev in seg_peers() + peers:
         pl.semaphore_signal(barrier, inc=1, device_id=dev, device_id_type=MESH)
 
     wins = ((k_ref, k_win), (v_ref, v_win), (q_ref, q_win), (g_ref, g_win))
@@ -320,8 +313,11 @@
                 part = pltpu.roll(part, 256 - (chans * o - begin), 1)
             taps = jnp.where(head == o, part, taps)
         w_own[i, 0:3] = taps
-    att[...] = jnp.zeros_like(att)
-    conv_in[...] = jnp.zeros_like(conv_in)
+    for f in range(FRAMES):
+        att[f, HEADS * D:, :] = jnp.zeros((32, WIN), F32)
+    conv_in[BASE + 800:, :] = jnp.zeros((WIN - 800, 256), F32)
+    for p in (SEGS - 2, SEGS - 1):
+        own[p] = jnp.zeros((PIECE, 128), F32)
 
     for f in range(FRAMES):
         loading(0, f).wait()
@@ -331,12 +327,11 @@
     for h in range(HEADS):
         for f in range(1, FRAMES):
             local[h, f] = local[h, f] + local[h, f - 1]
-        own[2 * h], own[2 * h + 1] = local[h, FRAMES - 1, :56], local[h, FRAMES - 1, 56:]
-    pl.semaphore_wait(barrier, 15)
-    scan = Scan(own, before, scratch[:6], False)
+        put_rows(own, h, local[h, FRAMES - 1])
+    pl.semaphore_wait(barrier, SEGS - 1 + 7)
+    scan = Scan(own, before, scratch[:4], False)
     scan.first()
     scan.second()
-    scan.third()
     scan.last()
 
     def state(h, f):
@@ -345,7 +340,7 @@
     for i, f in enumerate(ORDER):
         loading(2, f).wait()
         attend(f, q_win, state, att, inv)
-        convolve(f, att, conv_in, w_own, act)
+        convolve(f, att, conv_in, w_own, act, rest)
         for k in HOPS:
             strip(f, k).start()
         mine(f).start()
@@ -357,14 +352,12 @@
     for h in range(HEADS):
         for f in range(FRAMES - 2, -1, -1):
             ds[h, f] = ds[h, f] + ds[h, f + 1]
-        own[2 * h], own[2 * h + 1] = ds[h, 0, :56], ds[h, 0, 56:]
-    scan = Scan(own, after, scratch[6:], True)
+        put_rows(own, h, ds[h, 0])
+    scan = Scan(own, after, scratch[4:], True)
     scan.first()
-    pass_on(1)
+    pass_on(2)
     scan.second()
     pass_on(2)
-    scan.third()
-    pass_on(1)
     scan.last()
     pass_on(len(queue))
 
@@ -392,15 +385,15 @@
     wide = jax.ShapeDtypeStruct((HEADS * D, STRIDE * 3 + WIN), F32)
     window = pltpu.VMEM((FRAMES, HEADS * D, WIN), F32)
     states = pltpu.VMEM((HEADS, FRAMES, D, 128), F32)
-    quarters = pltpu.VMEM((4, 56, 128), F32)
+    pieces = pltpu.VMEM((SEGS, PIECE, 128), F32)
     return pl.pallas_call(
         main_kernel,
         out_shape=(
             wide,
             wide,
             wide,
-            jax.ShapeDtypeStruct((STRIPS, FRAMES, CELLS, 256), F32),
-            jax.ShapeDtypeStruct((STRIPS, 2, CELLS, 256), F32),
+            jax.ShapeDtypeStruct((STRIPS, FRAMES, PACKED, 128), F32),
+            jax.ShapeDtypeStruct((STRIPS, 2, PACKED, 128), F32),
         ),
         in_specs=[hbm] * 4 + [vmem],
         out_specs=(vmem, vmem, vmem, hbm, hbm),
@@ -409,9 +402,10 @@
             pltpu.VMEM((FRAMES, 256, WIN), F32),
             pltpu.VMEM((FRAMES, HEADS, 8, WIN), F32),
             pltpu.VMEM((BASE + WIN, 256), F32),
-            pltpu.VMEM((FRAMES, STRIPS, CELLS, 256), F32),
+            pltpu.VMEM((FRAMES, STRIPS, PACKED, 128), F32),
+            pltpu.VMEM((STRIPS, 24, 128), F32),
             pltpu.VMEM((3, 8, 256), F32),
-            states, states, quarters, quarters, quarters,
+            states, states, pieces, pieces, pieces,
             pltpu.SemaphoreType.DMA((4, FRAMES)),
             pltpu.SemaphoreType.DMA((FRAMES, 8)),
             pltpu.SemaphoreType.DMA((FRAMES, 8)),
@@ -419,22 +413,34 @@
             pltpu.SemaphoreType.DMA((2, 8)),
             pltpu.SemaphoreType.DMA((FRAMES,)),
         ] + SCAN_SCRATCH + SCAN_SCRATCH,
-        compiler_params=pltpu.CompilerParams(collective_id=0, has_side_effects=True, vmem_limit_bytes=46 << 20),
+        compiler_params=pltpu.CompilerParams(collective_id=0, has_side_effects=True, vmem_limit_bytes=MAIN_LIMIT),
         name="attention_exchange",
     )(q, k, v, g, weights)
 
 
-def mix_group(base, count, halo_on, got, halo, tw_ref, tmp, mixed_ref):
+def cells(ref, index, base, count, lane):
+    if lane == 0:
+        return ref[index + (pl.ds(SPLIT + base, count),)]
+    if not isinstance(base, int):
+        return ref[index + (pl.ds(base, count),)]
+    place = lax.broadcasted_iota(jnp.int32, (count, 128), 1)
+    parts = [
+        pltpu.roll(ref[index + (slice(24 * p + base - SPLIT, 24 * p + base - SPLIT + count),)], 32 + 32 * p, 1)
+        for p in range(3)
+    ]
+    return jnp.where(place < 32, parts[0], jnp.where(place < 64, parts[1], parts[2]))
+
+
+def mix_group(base, count, halo_on, got, halo, tw_ref, tmp):
     head = lax.axis_index("head")
     place = lax.broadcasted_iota(jnp.int32, (count, 128), 1)
     pending = [None] * FRAMES
     for owner in range(STRIPS):
         slot = head ^ owner
         for lane in range(2):
-            lanes = slice(128 * lane, 128 * lane + 128)
-            acts = [jnp.where(halo_on, halo[slot, i, pl.ds(base, count), lanes], 0.0) for i in range(2)]
-            acts += [got[slot, f, pl.ds(base, count), lanes] for f in range(FRAMES)]
-            w = [tw_ref[owner, i:i + 1, lanes] for i in range(3)]
+            acts = [jnp.where(halo_on, cells(halo, (slot, i), base, count, lane), 0.0) for i in range(2)]
+            acts += [cells(got, (slot, f), base, count, lane) for f in range(FRAMES)]
+            w = [tw_ref[owner, i:i + 1, 128 * lane:128 * lane + 128] for i in range(3)]
             width = 128 if lane == 0 else 96
             tile, shift = divmod(224 * owner + 128 * lane, 128)
             for f in range(FRAMES):
@@ -450,7 +456,19 @@
                     pending[f] = full
 
 
-def mix_kernel(got, halo, tw_ref, mixed_ref, tmp, tw):
+def mix_kernel(got_ref, halo, tw_ref, gq, gk, gv, gq_out, gk_out, gv_out, mixed_out, got, tmp, tw, mixed, gsem, sem, msem):
+    parts = [
+        pltpu.make_async_copy(got_ref.at[:, :, rows], got.at[:, :, rows], gsem.at[i])
+        for i, rows in enumerate((slice(0, SPLIT), slice(SPLIT, 120), slice(120, PACKED)))
+    ]
+    for c in parts:
+        c.start()
+    plain = [
+        pltpu.make_async_copy(src, dst, sem.at[i])
+        for i, (src, dst) in enumerate(((gq, gq_out), (gk, gk_out), (gv, gv_out)))
+    ]
+    for c in plain:
+        c.start()
     for owner in range(STRIPS):
         begin = min(224 * owner, 1792 - 256)
         part = tw_ref[:, begin:begin + 256]
@@ -459,36 +477,61 @@
         tw[owner, 0:3] = part
     halo_on = lax.axis_index("seg") > 0
 
-    def group(base, count):
-        mix_group(base, count, halo_on, got, halo, tw, tmp, mixed_ref)
+    def leaving(base, count, i):
+        rows = pl.ds(base, count)
+        return pltpu.make_async_copy(mixed.at[rows], mixed_out.at[rows], msem.at[i])
+
+    def group(base, count, g):
+        mix_group(base, count, halo_on, got, halo, tw, tmp)
         for i in range(count):
             for t in range(14):
-                mixed_ref[base + i, :, 128 * t:128 * t + 128] = tmp[t, 4 * i:4 * i + 4, :]
+                mixed[base + i, :, 128 * t:128 * t + 128] = tmp[t, 4 * i:4 * i + 4, :]
+        leaving(base, count, g).start()
 
     def step(i, carry):
-        group(pl.multiple_of(8 * i, 8), 8)
+        group(pl.multiple_of(8 * i, 8), 8, i)
         return carry
 
-    lax.fori_loop(0, 12, step, 0)
-    group(96, 4)
-
-
-def mix(got, halo, tw):
+    parts[0].wait()
+    parts[1].wait()
+    lax.fori_loop(0, 5, step, 0)
+    parts[2].wait()
+    lax.fori_loop(5, 10, step, 0)
+    group(80, 8, 10)
+    group(88, 8, 11)
+    group(96, 4, 12)
+    for g in range(13):
+        leaving(8 * g, 4 if g == 12 else 8, g).wait()
+    for c in plain:
+        c.wait()
+
+
+def mix(got, halo, tw, gq, gk, gv):
     vmem = pl.BlockSpec(memory_space=pltpu.VMEM)
+    hbm = pl.BlockSpec(memory_space=pl.ANY)
+    wide = jax.ShapeDtypeStruct(gq.shape, F32)
     return pl.pallas_call(
         mix_kernel,
-        out_shape=jax.ShapeDtypeStruct((CELLS, FRAMES, 1792), F32),
-        in_specs=[vmem] * 3,
-        out_specs=vmem,
-        scratch_shapes=[pltpu.VMEM((14, 32, 128), F32), pltpu.VMEM((STRIPS, 8, 256), F32)],
-        compiler_params=pltpu.CompilerParams(vmem_limit_bytes=24 << 20),
+        out_shape=(wide, wide, wide, jax.ShapeDtypeStruct((CELLS, FRAMES, 1792), F32)),
+        in_specs=[hbm] + [vmem] * 5,
+        out_specs=(hbm, hbm, hbm, hbm),
+        scratch_shapes=[
+            pltpu.VMEM((STRIPS, FRAMES, PACKED, 128), F32),
+            pltpu.VMEM((14, 32, 128), F32),
+            pltpu.VMEM((STRIPS, 8, 256), F32),
+            pltpu.VMEM((CELLS, FRAMES, 1792), F32),
+            pltpu.SemaphoreType.DMA((3,)),
+            pltpu.SemaphoreType.DMA((3,)),
+            pltpu.SemaphoreType.DMA((13,)),
+        ],
+        compiler_params=pltpu.CompilerParams(vmem_limit_bytes=MIX_LIMIT),
         name="mix",
-    )(got, halo, tw)
+    )(got, halo, tw, gq, gk, gv)
 
 
 def body(query_feat, key_feat, value_feat, grad_out, spatial_weight, temporal_weight):
     gq, gk, gv, got, halo = main_call(query_feat, key_feat, value_feat, grad_out, spatial_weight)
-    mixed = mix(got, halo, temporal_weight)
+    gq, gk, gv, mixed = mix(got, halo, temporal_weight, gq, gk, gv)
     mixed = jnp.transpose(mixed.reshape(ROWS, 5, FRAMES, STRIPS * HEADS * D), (2, 0, 1, 3))
     return gq, gk, gv, mixed
 

time: 79.8 us -> 66.9 us (0.84)
  local copies, waits for them, and re-layouts: 8.83 us -> 0.89 us
  Pallas kernels: 69 us -> 64.5 us
    pallas_call x1, Pallas kernels: 65.5 us -> 57.2 us  [main_call(): pl.pallas_call(main_kernel, out_shape=(wide, wide, wide, jax.ShapeDtypeSt...]
    unnamed x11 -> x4, local copies, waits for them, and re-layouts: 8.83 us -> 0.89 us
    pallas_call x1, Pallas kernels: 3.52 us -> 7.3 us  [mix(): pl.pallas_call(mix_kernel, out_shape=(wide, wide, wide, jax.ShapeDtypeStr...]
where the time goes in v2:
time: 66.9 us; the launch traced here: 66.2 us
  Pallas kernels  64.5 us (96%)
  local copies, waits for them, and re-layouts  0.89 us (1%)
  between operations  0.82 us (1%)
    pallas_call x1, Pallas kernels, main_call(): pl.pallas_call(main_kernel, out_shape=(wide, wide, wide, jax.ShapeDtypeSt...  57.2 us
    pallas_call x1, Pallas kernels, mix(): pl.pallas_call(mix_kernel, out_shape=(wide, wide, wide, jax.ShapeDtypeStr...  7.3 us

profile of v2, /device:TPU:2, one launch (start us, length us, event | category | flops | bytes accessed | tf_op | source)
XLA Modules:
  0.0 66.2 jit_solution(17942247109366235014)
XLA Ops:
  0.6 0.0 copy-start
  0.6 0.9 %copy-done = f32[3,3,1792]{2,1,0:T(4,128)S(1)} copy-done((f32[3,3,1792]{2,1,0:T(4,128)S(1)}, f32[3,3,1792]{2,1,0:T(4,128)}, u32[]{:S(2)}) %copy-start) | copy-done | bytes 64536
  1.5 0.0 copy-start.1
  1.5 57.2 %attention_exchange.1 = (f32[224,3200]{1,0:T(8,128)S(1)}, f32[224,3200]{1,0:T(8,128)S(1)}, f32[224,3200]{1,0:T(8,128)S(1)}, f32[8,4,180,128]{3,2,1,0:T(8,128)}, f32[8,2,180,128]{3,2,1,0:T(8,128)S(1)}) custom-call(f32[224,3200]{1,0:T(8,128)} %q_ref.1, f32[224,3200]{1,0:T(8,128)} %k_ref.1, f32[224,3200]{1,0:T(8,128)} %v_ref.1, f32[224,3200]{1,0:T(8,128)} %g_ref.1, ...), custom_call_target="tpu_custom_call" | custom-call | tf_op jit(solution)/shard_map/attention_exchange/pallas_call | solution.py:389
  58.7 0.0 copy-done.1
  58.8 7.3 %mix.1 = (f32[224,3200]{1,0:T(8,128)}, f32[224,3200]{1,0:T(8,128)}, f32[224,3200]{1,0:T(8,128)}, f32[100,4,1792]{2,1,0:T(4,128)}) custom-call(f32[8,4,180,128]{3,2,1,0:T(8,128)} %get-tuple-element.13.got_ref, f32[8,2,180,128]{3,2,1,0:T(8,128)S(1)} %get-tuple-element.14.halo, f32[3,1792]{1,0:T(4,128)S(1)} %copy-done.1, f32[224,3200]{1,0:T(8,128)S(1)} %get-tuple-element.15.gq, ...), custom_call_target="tpu_custom_call" | custom-call | tf_op jit(solution)/shard_map/mix/pallas_call | solution.py:513
Async XLA Ops:
  0.6 0.9 %copy-start = (f32[3,3,1792]{2,1,0:T(4,128)S(1)}, f32[3,3,1792]{2,1,0:T(4,128)}, u32[]{:S(2)}) copy-start(f32[3,3,1792]{2,1,0:T(4,128)} %sw_ref.1) | copy-start | bytes 193540
  1.5 57.2 %copy-start.1 = (f32[3,1792]{1,0:T(4,128)S(1)}, f32[3,1792]{1,0:T(4,128)}, u32[]{:S(2)}) copy-start(f32[3,1792]{1,0:T(4,128)} %tw_ref.1) | copy-start | bytes 64516

commit v3 on v2

--- a/solution.py
+++ b/solution.py
@@ -23,8 +23,8 @@
 MESH = pl.DeviceIdType.MESH
 F32 = jnp.float32
 BF16 = jnp.bfloat16
-MAIN_LIMIT = 43 << 20
-MIX_LIMIT = 43 << 20
+MAIN_LIMIT = 39 << 20
+MIX_LIMIT = 39 << 20
 
 
 def split(x):
@@ -115,7 +115,7 @@
 
     def second(self):
         for c in self.c1:
-            c.wait()
+            c.wait_recv()
         total = jnp.zeros((PIECE, 128), F32)
         order = range(SEGS - 1, -1, -1) if self.reverse else range(SEGS)
         for j in order:
@@ -130,7 +130,11 @@
 
     def last(self):
         for c in self.c2:
-            c.wait()
+            c.wait_recv()
+
+    def drain(self):
+        for c in self.c1 + self.c2:
+            c.wait_send()
 
 
 def ones_row(width):
@@ -254,7 +258,7 @@
 HOPS = (1, 2, 6, 3, 5, 7, 4)
 
 
-def main_kernel(q_ref, k_ref, v_ref, g_ref, sw_ref, gq_ref, gk_ref, gv_ref, got_ref, halo_ref,
+def main_kernel(q_ref, k_ref, v_ref, g_ref, sw_ref, gq_ref, gk_ref, gv_ref, got_early, got_late, halo_ref,
                 q_win, k_win, v_win, g_win, att, inv, conv_in, act, rest, w_own, local, ds, own, before, after,
                 load, send, recv, fsend, frecv, lsem, *scratch):
     seg, head = lax.axis_index("seg"), lax.axis_index("head")
@@ -273,25 +277,25 @@
     for f in range(FRAMES):
         for i in range(2):
             loading(i, f).start()
-    for i in (2, 3):
-        for f in ORDER:
-            loading(i, f).start()
+
+    def got_at(k, f):
+        return (got_early if f >= 2 else got_late).at[k, f % 2]
 
     def strip(f, k):
         return pltpu.make_async_remote_copy(
-            src_ref=act.at[f, head ^ k], dst_ref=got_ref.at[k, f], send_sem=send.at[f, k], recv_sem=recv.at[f, k],
+            src_ref=act.at[f, head ^ k], dst_ref=got_at(k, f), send_sem=send.at[f, k], recv_sem=recv.at[f, k],
             device_id=(seg, head ^ k), device_id_type=MESH,
         )
 
     def forward(f, k):
-        src = act.at[f, head] if k == 0 else got_ref.at[k, f]
+        src = act.at[f, head] if k == 0 else got_at(k, f)
         return pltpu.make_async_remote_copy(
             src_ref=src, dst_ref=halo_ref.at[k, f - 2], send_sem=fsend.at[f - 2, k], recv_sem=frecv.at[f - 2, k],
             device_id=up, device_id_type=MESH,
         )
 
     def mine(f):
-        return pltpu.make_async_copy(act.at[f, head], got_ref.at[0, f], lsem.at[f])
+        return pltpu.make_async_copy(act.at[f, head], got_at(0, f), lsem.at[f])
 
     queue = [(2, 0), (3, 0), (2, 1), (3, 1)] + [(2, k) for k in HOPS[1:]] + [(3, k) for k in HOPS[1:]]
 
@@ -302,6 +306,24 @@
             forward(f, k).start()
         del queue[:count]
 
+    for p in (SEGS - 2, SEGS - 1):
+        own[p] = jnp.zeros((PIECE, 128), F32)
+
+    for f in range(FRAMES):
+        loading(0, f).wait()
+        loading(1, f).wait()
+        for h in range(HEADS):
+            local[h, f] = sums_frame(h, f, k_win, v_win)
+    for h in range(HEADS):
+        for f in range(1, FRAMES):
+            local[h, f] = local[h, f] + local[h, f - 1]
+        put_rows(own, h, local[h, FRAMES - 1])
+    pl.semaphore_wait(barrier, SEGS - 1 + 7)
+    scan = Scan(own, before, scratch[:4], False)
+    scan.first()
+    for i in (2, 3):
+        for f in ORDER:
+            loading(i, f).start()
     lanes = pl.ds(0, 256)
     chans = HEADS * D
     for i in range(3):
@@ -316,21 +338,6 @@
     for f in range(FRAMES):
         att[f, HEADS * D:, :] = jnp.zeros((32, WIN), F32)
     conv_in[BASE + 800:, :] = jnp.zeros((WIN - 800, 256), F32)
-    for p in (SEGS - 2, SEGS - 1):
-        own[p] = jnp.zeros((PIECE, 128), F32)
-
-    for f in range(FRAMES):
-        loading(0, f).wait()
-        loading(1, f).wait()
-        for h in range(HEADS):
-            local[h, f] = sums_frame(h, f, k_win, v_win)
-    for h in range(HEADS):
-        for f in range(1, FRAMES):
-            local[h, f] = local[h, f] + local[h, f - 1]
-        put_rows(own, h, local[h, FRAMES - 1])
-    pl.semaphore_wait(barrier, SEGS - 1 + 7)
-    scan = Scan(own, before, scratch[:4], False)
-    scan.first()
     scan.second()
     scan.last()
 
@@ -348,7 +355,7 @@
     for i, f in enumerate(ORDER):
         loading(3, f).wait()
         query_grads(f, q_win, g_win, state, att, inv, gq_ref, ds)
-        pass_on((1, 0, 1, 0)[i])
+    scan.drain()
     for h in range(HEADS):
         for f in range(FRAMES - 2, -1, -1):
             ds[h, f] = ds[h, f] + ds[h, f + 1]
@@ -359,13 +366,16 @@
     scan.second()
     pass_on(2)
     scan.last()
-    pass_on(len(queue))
+    pass_on(4)
 
     def later(h, f):
         return rows_of(after, h) + ds[h, f]
 
     for f in range(FRAMES):
         key_grads(f, k_win, v_win, later, gk_ref, gv_ref)
+        pass_on(1)
+    pass_on(len(queue))
+    scan.drain()
     for f in range(FRAMES):
         mine(f).wait()
     for f in (0, 1):
@@ -383,6 +393,7 @@
     hbm = pl.BlockSpec(memory_space=pl.ANY)
     vmem = pl.BlockSpec(memory_space=pltpu.VMEM)
     wide = jax.ShapeDtypeStruct((HEADS * D, STRIDE * 3 + WIN), F32)
+    half = jax.ShapeDtypeStruct((STRIPS, 2, PACKED, 128), F32)
     window = pltpu.VMEM((FRAMES, HEADS * D, WIN), F32)
     states = pltpu.VMEM((HEADS, FRAMES, D, 128), F32)
     pieces = pltpu.VMEM((SEGS, PIECE, 128), F32)
@@ -392,11 +403,12 @@
             wide,
             wide,
             wide,
-            jax.ShapeDtypeStruct((STRIPS, FRAMES, PACKED, 128), F32),
-            jax.ShapeDtypeStruct((STRIPS, 2, PACKED, 128), F32),
+            half,
+            half,
+            half,
         ),
         in_specs=[hbm] * 4 + [vmem],
-        out_specs=(vmem, vmem, vmem, hbm, hbm),
+        out_specs=(vmem, vmem, vmem, hbm, hbm, hbm),
         scratch_shapes=[
             window, window, window, window,
             pltpu.VMEM((FRAMES, 256, WIN), F32),
@@ -439,7 +451,7 @@
         slot = head ^ owner
         for lane in range(2):
             acts = [jnp.where(halo_on, cells(halo, (slot, i), base, count, lane), 0.0) for i in range(2)]
-            acts += [cells(got, (slot, f), base, count, lane) for f in range(FRAMES)]
+            acts += [cells(got[f // 2], (slot, f % 2), base, count, lane) for f in range(FRAMES)]
             w = [tw_ref[owner, i:i + 1, 128 * lane:128 * lane + 128] for i in range(3)]
             width = 128 if lane == 0 else 96
             tile, shift = divmod(224 * owner + 128 * lane, 128)
@@ -456,13 +468,7 @@
                     pending[f] = full
 
 
-def mix_kernel(got_ref, halo, tw_ref, gq, gk, gv, gq_out, gk_out, gv_out, mixed_out, got, tmp, tw, mixed, gsem, sem, msem):
-    parts = [
-        pltpu.make_async_copy(got_ref.at[:, :, rows], got.at[:, :, rows], gsem.at[i])
-        for i, rows in enumerate((slice(0, SPLIT), slice(SPLIT, 120), slice(120, PACKED)))
-    ]
-    for c in parts:
-        c.start()
+def mix_kernel(got_early, got_late, halo, tw_ref, gq, gk, gv, gq_out, gk_out, gv_out, mixed_out, tmp, tw, mixed, sem, msem):
     plain = [
         pltpu.make_async_copy(src, dst, sem.at[i])
         for i, (src, dst) in enumerate(((gq, gq_out), (gk, gk_out), (gv, gv_out)))
@@ -482,7 +488,7 @@
         return pltpu.make_async_copy(mixed.at[rows], mixed_out.at[rows], msem.at[i])
 
     def group(base, count, g):
-        mix_group(base, count, halo_on, got, halo, tw, tmp)
+        mix_group(base, count, halo_on, (got_late, got_early), halo, tw, tmp)
         for i in range(count):
             for t in range(14):
                 mixed[base + i, :, 128 * t:128 * t + 128] = tmp[t, 4 * i:4 * i + 4, :]
@@ -492,11 +498,7 @@
         group(pl.multiple_of(8 * i, 8), 8, i)
         return carry
 
-    parts[0].wait()
-    parts[1].wait()
-    lax.fori_loop(0, 5, step, 0)
-    parts[2].wait()
-    lax.fori_loop(5, 10, step, 0)
+    lax.fori_loop(0, 10, step, 0)
     group(80, 8, 10)
     group(88, 8, 11)
     group(96, 4, 12)
@@ -506,32 +508,30 @@
         c.wait()
 
 
-def mix(got, halo, tw, gq, gk, gv):
+def mix(early, late, halo, tw, gq, gk, gv):
     vmem = pl.BlockSpec(memory_space=pltpu.VMEM)
     hbm = pl.BlockSpec(memory_space=pl.ANY)
     wide = jax.ShapeDtypeStruct(gq.shape, F32)
     return pl.pallas_call(
         mix_kernel,
         out_shape=(wide, wide, wide, jax.ShapeDtypeStruct((CELLS, FRAMES, 1792), F32)),
-        in_specs=[hbm] + [vmem] * 5,
+        in_specs=[vmem] * 7,
         out_specs=(hbm, hbm, hbm, hbm),
         scratch_shapes=[
-            pltpu.VMEM((STRIPS, FRAMES, PACKED, 128), F32),
             pltpu.VMEM((14, 32, 128), F32),
             pltpu.VMEM((STRIPS, 8, 256), F32),
             pltpu.VMEM((CELLS, FRAMES, 1792), F32),
-            pltpu.SemaphoreType.DMA((3,)),
             pltpu.SemaphoreType.DMA((3,)),
             pltpu.SemaphoreType.DMA((13,)),
         ],
         compiler_params=pltpu.CompilerParams(vmem_limit_bytes=MIX_LIMIT),
         name="mix",
-    )(got, halo, tw, gq, gk, gv)
+    )(early, late, halo, tw, gq, gk, gv)
 
 
 def body(query_feat, key_feat, value_feat, grad_out, spatial_weight, temporal_weight):
-    gq, gk, gv, got, halo = main_call(query_feat, key_feat, value_feat, grad_out, spatial_weight)
-    gq, gk, gv, mixed = mix(got, halo, temporal_weight, gq, gk, gv)
+    gq, gk, gv, early, late, halo = main_call(query_feat, key_feat, value_feat, grad_out, spatial_weight)
+    gq, gk, gv, mixed = mix(early, late, halo, temporal_weight, gq, gk, gv)
     mixed = jnp.transpose(mixed.reshape(ROWS, 5, FRAMES, STRIPS * HEADS * D), (2, 0, 1, 3))
     return gq, gk, gv, mixed
 

time: 66.9 us -> 64.5 us (0.964)
  Pallas kernels: 64.5 us -> 61.5 us
    pallas_call x1, Pallas kernels: 7.3 us -> 4.37 us  [mix(): pl.pallas_call(mix_kernel, out_shape=(wide, wide, wide, jax.ShapeDtypeStr...]
where the time goes in v3:
time: 64.5 us; the launch traced here: 63.2 us
  Pallas kernels  61.5 us (95%)
  local copies, waits for them, and re-layouts  0.89 us (1%)
  between operations  0.82 us (1%)
    pallas_call x1, Pallas kernels, main_call(): pl.pallas_call(main_kernel, out_shape=(wide, wide, wide, half, half, half...  57.1 us
    pallas_call x1, Pallas kernels, mix(): pl.pallas_call(mix_kernel, out_shape=(wide, wide, wide, jax.ShapeDtypeStr...  4.37 us

profile of v3, /device:TPU:2, one launch (start us, length us, event | category | flops | bytes accessed | tf_op | source)
XLA Modules:
  0.0 63.2 jit_solution(11588920866723572365)
XLA Ops:
  0.6 0.0 copy-start
  0.6 0.9 %copy-done = f32[3,3,1792]{2,1,0:T(4,128)S(1)} copy-done((f32[3,3,1792]{2,1,0:T(4,128)S(1)}, f32[3,3,1792]{2,1,0:T(4,128)}, u32[]{:S(2)}) %copy-start) | copy-done | bytes 64536
  1.5 0.0 copy-start.1
  1.5 57.1 %attention_exchange.1 = (f32[224,3200]{1,0:T(8,128)S(1)}, f32[224,3200]{1,0:T(8,128)S(1)}, f32[224,3200]{1,0:T(8,128)S(1)}, f32[8,2,180,128]{3,2,1,0:T(8,128)S(1...) custom-call(f32[224,3200]{1,0:T(8,128)} %q_ref.1, f32[224,3200]{1,0:T(8,128)} %k_ref.1, ...), custom_call_target="tpu_custom_call" | custom-call | tf_op jit(solution)/shard_map/attention_exchange/pallas_call | solution.py:400
  58.7 0.0 copy-done.1
  58.7 4.4 %mix.1 = (f32[224,3200]{1,0:T(8,128)}, f32[224,3200]{1,0:T(8,128)}, f32[224,3200]{1,0:T(8,128)}, f32[100,4,1792]{2,1,0:T(4,128)}) custom-call(f32[8,2,180,128]{3,2,1,0:T(8,128)S(1)} %get-tuple-element.14.got_early, f32[8,2,180,128]{3,2,1,0:T(8,128)S(1)} %get-tuple-element.15.got_late, f32[8,2,180,128]{3,2,1,0:T(8,128)S(1)} %get-tuple-element.16.halo, ...), custom_call_target="tpu_custom_call" | custom-call | tf_op jit(solution)/shard_map/mix/pallas_call | solution.py:515
Async XLA Ops:
  0.6 0.9 %copy-start = (f32[3,3,1792]{2,1,0:T(4,128)S(1)}, f32[3,3,1792]{2,1,0:T(4,128)}, u32[]{:S(2)}) copy-start(f32[3,3,1792]{2,1,0:T(4,128)} %sw_ref.1) | copy-start | bytes 193540
  1.5 57.1 %copy-start.1 = (f32[3,1792]{1,0:T(4,128)S(1)}, f32[3,1792]{1,0:T(4,128)}, u32[]{:S(2)}) copy-start(f32[3,1792]{1,0:T(4,128)} %tw_ref.1) | copy-start | bytes 64516

commit v4 on v3

--- a/solution.py
+++ b/solution.py
@@ -256,11 +256,12 @@
 
 ORDER = (2, 3, 0, 1)
 HOPS = (1, 2, 6, 3, 5, 7, 4)
+RELAYED = ((3, 0), (2, 1), (3, 1))
 
 
 def main_kernel(q_ref, k_ref, v_ref, g_ref, sw_ref, gq_ref, gk_ref, gv_ref, got_early, got_late, halo_ref,
                 q_win, k_win, v_win, g_win, att, inv, conv_in, act, rest, w_own, local, ds, own, before, after,
-                load, send, recv, fsend, frecv, lsem, *scratch):
+                load, send, recv, fsend, frecv, lsem, relay, rsend, rrecv, *scratch):
     seg, head = lax.axis_index("seg"), lax.axis_index("head")
     peers = [(seg, head ^ k) for k in range(1, 8)]
     up = ((seg + 1) % SEGS, head)
@@ -297,13 +298,43 @@
     def mine(f):
         return pltpu.make_async_copy(act.at[f, head], got_at(0, f), lsem.at[f])
 
-    queue = [(2, 0), (3, 0), (2, 1), (3, 1)] + [(2, k) for k in HOPS[1:]] + [(3, k) for k in HOPS[1:]]
+    x, y = seg // 4, seg % 4
+    below = (4 * x + (y + 3) % 4, head)
+    beyond = ((4 * x + (y + 2) % 4 + 1) % SEGS, head)
+
+    def detour(leg, i):
+        f, k = RELAYED[i]
+        if leg == 0:
+            src = act.at[f, head] if k == 0 else got_at(k, f)
+        else:
+            src = relay.at[leg - 1, i]
+        dst, sem = (halo_ref.at[k, f - 2], frecv.at[f - 2, k]) if leg == 2 else (relay.at[leg, i], rrecv.at[leg, i])
+        return pltpu.make_async_remote_copy(
+            src_ref=src, dst_ref=dst, send_sem=rsend.at[leg, i], recv_sem=sem,
+            device_id=beyond if leg == 2 else below, device_id_type=MESH,
+        )
+
+    def take_detour(leg, i):
+        f, k = RELAYED[i]
+        if leg == 0 and k:
+            strip(f, k).wait_recv()
+
+        @pl.when(seg != SEGS - 1 - leg)
+        def _():
+            if leg:
+                detour(leg - 1, i).wait_recv()
+            detour(leg, i).start()
+
+    queue = [(2, 0)] + [(2, k) for k in HOPS[1:]] + [(3, k) for k in HOPS[1:]]
 
     def pass_on(count):
         for f, k in queue[:count]:
             if k:
                 strip(f, k).wait_recv()
-            forward(f, k).start()
+
+            @pl.when(seg != SEGS - 1)
+            def _():
+                forward(f, k).start()
         del queue[:count]
 
     for p in (SEGS - 2, SEGS - 1):
@@ -351,7 +382,12 @@
         for k in HOPS:
             strip(f, k).start()
         mine(f).start()
-        pass_on((1, 2, 2, 2)[i])
+        pass_on((1, 0, 2, 2)[i])
+        if i == 1:
+            take_detour(0, 0)
+            take_detour(0, 1)
+        if i == 2:
+            take_detour(0, 2)
     for i, f in enumerate(ORDER):
         loading(3, f).wait()
         query_grads(f, q_win, g_win, state, att, inv, gq_ref, ds)
@@ -363,10 +399,15 @@
     scan = Scan(own, after, scratch[4:], True)
     scan.first()
     pass_on(2)
+    for i in range(3):
+        take_detour(1, i)
+    pass_on(2)
     scan.second()
     pass_on(2)
+    for i in range(3):
+        take_detour(2, i)
+    pass_on(1)
     scan.last()
-    pass_on(4)
 
     def later(h, f):
         return rows_of(after, h) + ds[h, f]
@@ -386,7 +427,14 @@
             strip(f, k).wait_send()
     for f in (2, 3):
         for k in (0,) + HOPS:
-            forward(f, k).wait()
+            if (f, k) in RELAYED:
+                i = RELAYED.index((f, k))
+                for leg in range(3):
+                    pl.when(seg != SEGS - 1 - leg)(detour(leg, i).wait_send)
+                pl.when(seg != 0)(detour(2, i).wait_recv)
+            else:
+                pl.when(seg != SEGS - 1)(forward(f, k).wait_send)
+                pl.when(seg != 0)(forward(f, k).wait_recv)
 
 
 def main_call(q, k, v, g, weights):
@@ -424,6 +472,9 @@
             pltpu.SemaphoreType.DMA((2, 8)),
             pltpu.SemaphoreType.DMA((2, 8)),
             pltpu.SemaphoreType.DMA((FRAMES,)),
+            pltpu.VMEM((2, 3, PACKED, 128), F32),
+            pltpu.SemaphoreType.DMA((3, 3)),
+            pltpu.SemaphoreType.DMA((2, 3)),
         ] + SCAN_SCRATCH + SCAN_SCRATCH,
         compiler_params=pltpu.CompilerParams(collective_id=0, has_side_effects=True, vmem_limit_bytes=MAIN_LIMIT),
         name="attention_exchange",

time: 64.5 us -> 62.3 us (0.966); the launches traced: 63.2 us -> 62.1 us
  Pallas kernels: 61.5 us -> 60.4 us
    pallas_call x1, Pallas kernels: 57.1 us -> 56 us  [main_call(): pl.pallas_call(main_kernel, out_shape=(wide, wide, wide, half, half, half...]
where the time goes in v4:
time: 62.3 us; the launch traced here: 62.1 us
  Pallas kernels  60.4 us (97%)
  local copies, waits for them, and re-layouts  0.89 us (1%)
  between operations  0.82 us (1%)
    pallas_call x1, Pallas kernels, main_call(): pl.pallas_call(main_kernel, out_shape=(wide, wide, wide, half, half, half...  56 us
    pallas_call x1, Pallas kernels, mix(): pl.pallas_call(mix_kernel, out_shape=(wide, wide, wide, jax.ShapeDtypeStr...  4.37 us

profile of v4, /device:TPU:2, one launch (start us, length us, event | category | flops | bytes accessed | tf_op | source)
XLA Modules:
  0.0 62.1 jit_solution(14177425481780613354)
XLA Ops:
  0.6 0.0 copy-start
  0.6 0.9 %copy-done = f32[3,3,1792]{2,1,0:T(4,128)S(1)} copy-done((f32[3,3,1792]{2,1,0:T(4,128)S(1)}, f32[3,3,1792]{2,1,0:T(4,128)}, u32[]{:S(2)}) %copy-start) | copy-done | bytes 64536
  1.5 0.0 copy-start.1
  1.5 56.0 %attention_exchange.1 = (f32[224,3200]{1,0:T(8,128)S(1)}, f32[224,3200]{1,0:T(8,128)S(1)}, f32[224,3200]{1,0:T(8,128)S(1)}, f32[8,2,180,128]{3,2,1,0:T(8,128)S(1...) custom-call(f32[224,3200]{1,0:T(8,128)} %q_ref.1, f32[224,3200]{1,0:T(8,128)} %k_ref.1, ...), custom_call_target="tpu_custom_call" | custom-call | tf_op jit(solution)/shard_map/attention_exchange/pallas_call | solution.py:448
  57.6 0.0 copy-done.1
  57.6 4.4 %mix.1 = (f32[224,3200]{1,0:T(8,128)}, f32[224,3200]{1,0:T(8,128)}, f32[224,3200]{1,0:T(8,128)}, f32[100,4,1792]{2,1,0:T(4,128)}) custom-call(f32[8,2,180,128]{3,2,1,0:T(8,128)S(1)} %get-tuple-element.14.got_early, f32[8,2,180,128]{3,2,1,0:T(8,128)S(1)} %get-tuple-element.15.got_late, f32[8,2,180,128]{3,2,1,0:T(8,128)S(1)} %get-tuple-element.16.halo, ...), custom_call_target="tpu_custom_call" | custom-call | tf_op jit(solution)/shard_map/mix/pallas_call | solution.py:566
Async XLA Ops:
  0.6 0.9 %copy-start = (f32[3,3,1792]{2,1,0:T(4,128)S(1)}, f32[3,3,1792]{2,1,0:T(4,128)}, u32[]{:S(2)}) copy-start(f32[3,3,1792]{2,1,0:T(4,128)} %sw_ref.1) | copy-start | bytes 193540
  1.5 56.1 %copy-start.1 = (f32[3,1792]{1,0:T(4,128)S(1)}, f32[3,1792]{1,0:T(4,128)}, u32[]{:S(2)}) copy-start(f32[3,1792]{1,0:T(4,128)} %tw_ref.1) | copy-start | bytes 64516

commit v5 on v4

--- a/solution.py
+++ b/solution.py
@@ -16,8 +16,10 @@
 HEADS = 2
 STRIPS = 8
 CELLS = 100
-SPLIT = 80
-PACKED = SPLIT + CELLS
+SECOND = 104
+PLAIN = 72
+REST = 76
+PACKED = SECOND + PLAIN
 CHUNKS = ((0, 256), (256, 256), (512, 256), (768, 128))
 BASE = 136
 MESH = pl.DeviceIdType.MESH
@@ -197,15 +199,18 @@
             for j in range(STRIPS):
                 part = act[5 * j:5 * j + 5]
                 if lane == 0:
-                    send[f, j, SPLIT + 5 * r:SPLIT + 5 * r + 5, :] = part
-                elif 5 * r < SPLIT:
                     send[f, j, 5 * r:5 * r + 5, :] = part
-                else:
-                    rest[j, 5 * r - SPLIT:5 * r - SPLIT + 5, :] = part
+                    continue
+                for low, high, to in ((0, PLAIN, SECOND), (PLAIN, REST, CELLS), (REST, CELLS, None)):
+                    a, b = max(5 * r, low), min(5 * r + 5, high)
+                    if a < b and to is None:
+                        rest[j, a - REST:b - REST, :] = part[a - 5 * r:b - 5 * r]
+                    elif a < b:
+                        send[f, j, to + a - low:to + b - low, :] = part[a - 5 * r:b - 5 * r]
     free = lax.broadcasted_iota(jnp.int32, (24, 128), 1) >= 96
     for j in range(STRIPS):
         for p in range(3):
-            rows = slice(24 * p, 24 * p + 24)
+            rows = slice(SECOND + 24 * p, SECOND + 24 * p + 24)
             send[f, j, rows, :] = jnp.where(free, pltpu.roll(rest[j], 96 - 32 * p, 1), send[f, j, rows, :])
 
 
@@ -256,6 +261,7 @@
 
 ORDER = (2, 3, 0, 1)
 HOPS = (1, 2, 6, 3, 5, 7, 4)
+FAR_FIRST = (4, 5, 2, 6, 3, 7, 1)
 RELAYED = ((3, 0), (2, 1), (3, 1))
 
 
@@ -379,7 +385,7 @@
         loading(2, f).wait()
         attend(f, q_win, state, att, inv)
         convolve(f, att, conv_in, w_own, act, rest)
-        for k in HOPS:
+        for k in HOPS if f >= 2 else FAR_FIRST:
             strip(f, k).start()
         mine(f).start()
         pass_on((1, 0, 2, 2)[i])
@@ -483,15 +489,20 @@
 
 def cells(ref, index, base, count, lane):
     if lane == 0:
-        return ref[index + (pl.ds(SPLIT + base, count),)]
+        return ref[index + (pl.ds(base, count),)]
     if not isinstance(base, int):
-        return ref[index + (pl.ds(base, count),)]
+        return ref[index + (pl.ds(SECOND + base, count),)]
     place = lax.broadcasted_iota(jnp.int32, (count, 128), 1)
+    begin = max(base - REST, -4)
     parts = [
-        pltpu.roll(ref[index + (slice(24 * p + base - SPLIT, 24 * p + base - SPLIT + count),)], 32 + 32 * p, 1)
+        pltpu.roll(ref[index + (slice(SECOND + 24 * p + begin, SECOND + 24 * p + begin + count),)], 32 + 32 * p, 1)
         for p in range(3)
     ]
-    return jnp.where(place < 32, parts[0], jnp.where(place < 64, parts[1], parts[2]))
+    value = jnp.where(place < 32, parts[0], jnp.where(place < 64, parts[1], parts[2]))
+    if begin < 0:
+        row = lax.broadcasted_iota(jnp.int32, (count, 128), 0)
+        value = jnp.where(row < 4, ref[index + (slice(CELLS, CELLS + count),)], value)
+    return value
 
 
 def mix_group(base, count, halo_on, got, halo, tw_ref, tmp):
@@ -549,7 +560,8 @@
         group(pl.multiple_of(8 * i, 8), 8, i)
         return carry
 
-    lax.fori_loop(0, 10, step, 0)
+    lax.fori_loop(0, 9, step, 0)
+    group(72, 8, 9)
     group(80, 8, 10)
     group(88, 8, 11)
     group(96, 4, 12)

time: 62.3 us -> 61.9 us (level)
  no operation moved by 1% of the time
where the time goes in v5:
time: 61.9 us; the launch traced here: 61.8 us
  Pallas kernels  60.1 us (97%)
  local copies, waits for them, and re-layouts  0.89 us (1%)
  between operations  0.82 us (1%)
    pallas_call x1, Pallas kernels, main_call(): pl.pallas_call(main_kernel, out_shape=(wide, wide, wide, half, half, half...  55.5 us
    pallas_call x1, Pallas kernels, mix(): pl.pallas_call(mix_kernel, out_shape=(wide, wide, wide, jax.ShapeDtypeStr...  4.53 us

profile of v5, /device:TPU:2, one launch (start us, length us, event | category | flops | bytes accessed | tf_op | source)
XLA Modules:
  0.0 61.8 jit_solution(15899897233649064065)
XLA Ops:
  0.6 0.0 copy-start
  0.6 0.9 %copy-done = f32[3,3,1792]{2,1,0:T(4,128)S(1)} copy-done((f32[3,3,1792]{2,1,0:T(4,128)S(1)}, f32[3,3,1792]{2,1,0:T(4,128)}, u32[]{:S(2)}) %copy-start) | copy-done | bytes 64536
  1.5 0.0 copy-start.1
  1.5 55.5 %attention_exchange.1 = (f32[224,3200]{1,0:T(8,128)S(1)}, f32[224,3200]{1,0:T(8,128)S(1)}, f32[224,3200]{1,0:T(8,128)S(1)}, f32[8,2,176,128]{3,2,1,0:T(8,128)S(1...) custom-call(f32[224,3200]{1,0:T(8,128)} %q_ref.1, f32[224,3200]{1,0:T(8,128)} %k_ref.1, ...), custom_call_target="tpu_custom_call" | custom-call | tf_op jit(solution)/shard_map/attention_exchange/pallas_call | solution.py:454
  57.1 0.0 copy-done.1
  57.1 4.5 %mix.1 = (f32[224,3200]{1,0:T(8,128)}, f32[224,3200]{1,0:T(8,128)}, f32[224,3200]{1,0:T(8,128)}, f32[100,4,1792]{2,1,0:T(4,128)}) custom-call(f32[8,2,176,128]{3,2,1,0:T(8,128)S(1)} %get-tuple-element.14.got_early, f32[8,2,176,128]{3,2,1,0:T(8,128)S(1)} %get-tuple-element.15.got_late, f32[8,2,176,128]{3,2,1,0:T(8,128)S(1)} %get-tuple-element.16.halo, ...), custom_call_target="tpu_custom_call" | custom-call | tf_op jit(solution)/shard_map/mix/pallas_call | solution.py:578
Async XLA Ops:
  0.6 0.9 %copy-start = (f32[3,3,1792]{2,1,0:T(4,128)S(1)}, f32[3,3,1792]{2,1,0:T(4,128)}, u32[]{:S(2)}) copy-start(f32[3,3,1792]{2,1,0:T(4,128)} %sw_ref.1) | copy-start | bytes 193540
  1.5 55.6 %copy-start.1 = (f32[3,1792]{1,0:T(4,128)S(1)}, f32[3,1792]{1,0:T(4,128)}, u32[]{:S(2)}) copy-start(f32[3,1792]{1,0:T(4,128)} %tw_ref.1) | copy-start | bytes 64516
